TPU v7x, 256 devices: a whole 4x4x8 slice. The times are simulated.
256 devices in a mesh: tm: 16 (over x_lo, z), row: 4 (over y), col: 4 (over x_hi, core).
Axes of the slice: x: 4 (x_hi: 2, x_lo: 2; x = x_hi * 2 + x_lo), y: 4, z: 8, core: 2. Of those that a mesh axis runs over, the one named last changes fastest.
Arguments:
- resid: bfloat16 [16, 48, 160, 1152], P('tm', 'row', 'col'), may hold values from -8 to 8
- spatial_qkv: bfloat16 [3, 16, 48, 160, 1152], P(None, 'tm', 'row', 'col'), may hold values from -12 to 12
- key_keep: int32 [16, 48, 160], P('tm', 'row', 'col'), may hold values 0 or 1
- w_spatial_out: bfloat16 [1152, 1152], replicated, may hold values from -0.1875 to 0.1875
- modulation: float32 [2, 1152], replicated, may hold values from -3 to 3
- w_temporal_qkv: bfloat16 [1152, 3456], replicated, may hold values from -4 to 4
Outputs:
- temporal_heads: bfloat16 [16, 48, 160, 1152], P('tm', 'row', 'col')
All inputs are finite; a program needn't handle non-finite values. No bound on the sum of `key_keep` on one device may be relied on, other than what follows from the above.
Results may differ from a plain program's by a relative error of at most 0.0084.
Values may be sent and summed in bfloat16 or wider, within the bound.
A program may use at most 128 MiB of HBM per device.

v0:
```python
import jax
import jax.numpy as jnp
from jax import lax
from jax.sharding import PartitionSpec as P

HEADS = 16
RADIUS = 3


NEG_FILL = -1e30
EPSILON = 1e-06


def extended(array, sides, width):
    for axis, dim in sides:
        count, length = (lax.axis_size(axis), array.shape[dim])
        up = [(i, (i + 1) % count) for i in range(count - 1)]
        down = [(j, i) for i, j in up]
        last = lax.slice_in_dim(array, length - width, length, axis=dim)
        leading = lax.slice_in_dim(array, 0, width, axis=dim)
        before = lax.ppermute(last, axis, up)
        after = lax.ppermute(leading, axis, down)
        array = jnp.concatenate([before, array, after], axis=dim)
    return array


def softmax_parts(scores, allowed):
    masked = jnp.where(allowed, scores, NEG_FILL)
    top_score = jnp.max(masked, -1, keepdims=True)
    weights_f = jnp.where(allowed, jnp.exp(masked - top_score), 0.0)
    return (weights_f.astype(jnp.bfloat16), jnp.sum(weights_f, -1))


def frame_attend(gathered, head_count):
    frames_all, single, items, width_three = gathered.shape
    width = width_three // 3
    head_size = width // head_count
    split_qkv = gathered.reshape(frames_all, items, 3, head_count, head_size)
    scores = jnp.einsum(
        "fphd,gphd->phfg",
        split_qkv[:, :, 0],
        split_qkv[:, :, 1],
        preferred_element_type=jnp.float32,
    ) * head_size ** (-0.5)
    weights_b, totals = softmax_parts(scores, True)
    weighted = jnp.einsum(
        "phfg,gphd->fphd", weights_b, split_qkv[:, :, 2], preferred_element_type=jnp.float32
    )
    result = weighted / jnp.transpose(totals, (2, 0, 1))[..., None]
    return result.astype(jnp.bfloat16).reshape(frames_all, single, items, width)


def per_device(resid, spatial_qkv, key_keep, w_spatial_out, modulation, w_temporal_qkv):
    frame_count, tile_rows, tile_cols, width = resid.shape
    head_size = width // HEADS
    score_scale = head_size ** (-0.5)
    tile_tokens = tile_rows * tile_cols
    pair = spatial_qkv[1:3]
    keep_flags = key_keep.astype(jnp.bfloat16)[None, :, :, :, None]
    padded_pair, padded_keep = (
        extended(pair, (("row", 2), ("col", 3)), RADIUS),
        extended(keep_flags, (("row", 2), ("col", 3)), RADIUS),
    )
    pad_rows = tile_rows + 2 * RADIUS
    pad_cols = tile_cols + 2 * RADIUS
    key_count = pad_rows * pad_cols
    queries = spatial_qkv[0].reshape(frame_count, tile_tokens, HEADS, head_size)
    keys_pad = padded_pair[0].reshape(frame_count, key_count, HEADS, head_size)
    values_pad = padded_pair[1].reshape(frame_count, key_count, HEADS, head_size)
    query_index = jnp.arange(tile_tokens)
    query_row = query_index // tile_cols
    query_col = query_index % tile_cols
    key_index = jnp.arange(key_count)
    key_row = key_index // pad_cols
    key_col = key_index % pad_cols
    row_gap = key_row[None, :] - query_row[:, None] - RADIUS
    col_gap = key_col[None, :] - query_col[:, None] - RADIUS
    in_window = (jnp.abs(row_gap) <= RADIUS) & (jnp.abs(col_gap) <= RADIUS)
    itself = (row_gap == 0) & (col_gap == 0)
    key_live = padded_keep.reshape(frame_count, key_count) > 0.5
    allowed = (in_window[None] & (key_live[:, None, :] | itself[None]))[:, None]
    scores = (
        jnp.einsum("fqhd,fkhd->fhqk", queries, keys_pad, preferred_element_type=jnp.float32)
        * score_scale
    )
    weights_b, totals = softmax_parts(scores, allowed)
    weighted = jnp.einsum(
        "fhqk,fkhd->fqhd", weights_b, values_pad, preferred_element_type=jnp.float32
    )
    spatial_heads = (weighted / jnp.transpose(totals, (0, 2, 1))[..., None]).astype(jnp.bfloat16)
    spatial_heads = spatial_heads.reshape(frame_count * tile_tokens, width)
    stream = resid.reshape(frame_count * tile_tokens, width).astype(jnp.float32) + jnp.dot(
        spatial_heads, w_spatial_out, preferred_element_type=jnp.float32
    )
    average = jnp.mean(stream, -1, keepdims=True)
    centered = stream - average
    variance = jnp.mean(centered * centered, -1, keepdims=True)
    normed = (
        centered * lax.rsqrt(variance + EPSILON) * (1.0 + modulation[1]) + modulation[0]
    ).astype(jnp.bfloat16)
    tm_count = lax.axis_size("tm")
    part_tokens = tile_tokens // tm_count
    projected = jnp.dot(normed, w_temporal_qkv, preferred_element_type=jnp.float32).astype(
        jnp.bfloat16
    )
    projected = projected.reshape(frame_count, tm_count, part_tokens, 3 * width)
    result = lax.all_to_all(
        frame_attend(
            lax.all_to_all(projected, "tm", split_axis=1, concat_axis=0, tiled=True), HEADS
        ),
        "tm",
        split_axis=0,
        concat_axis=1,
        tiled=True,
    )
    return result.reshape(frame_count, tile_rows, tile_cols, width)


def solution(mesh):
    return jax.shard_map(
        per_device,
        mesh=mesh,
        in_specs=(
            P("tm", "row", "col", None),
            P(None, "tm", "row", "col", None),
            P("tm", "row", "col"),
            P(),
            P(),
            P(),
        ),
        out_specs=P("tm", "row", "col", None),
        check_vma=False,
    )
```

profile of v0, /device:TPU:1, one launch (start us, length us, event | category | flops | bytes accessed | tf_op | source)
XLA Modules:
  0.0 271.1 jit_solution(14642412991492366859)
XLA Ops:
  0.9 4.0 %collective-permute-start.4 = (bf16[1,1,3,40,1]{3,2,4,1,0:T(4,128)(2,1)S(1)}, bf16[1,1,3,40,1]{3,2,4,1,0:T(4,128)(2,1)S(1)}, u32[]{:S(2)}, u32[]{:S(2)}) collective-permute-start(bf16[1,1,3,40,1]{3,2,4,1,0:T(4,128)(2,1)S(1)} %get-tuple-element.18), channel_id=1, source_target_pairs={{0,4},{4,8},{8,12},{1,5},{5,9},{9,13},{2,6},{6,10},{10,14},{3,7},{... | collective-permute-start | bytes 728 | tf_op jit(solution)/shard_map/ppermute | solution.py:21
  6.2 2.3 fusion.62
  8.5 5.0 %collective-permute-start = (bf16[2,1,3,40,1152]{4,3,2,1,0:T(8,128)(2,1)}, bf16[2,1,3,40,1152]{4,3,2,1,0:T(8,128)(2,1)}, u32[]{:S(2)}, u32[]{:S(2)}) collective-permute-start(bf16[2,1,3,40,1152]{4,3,2,1,0:T(8,128)(2,1)} %get-tuple-element.14), channel_id=1, source_target_pairs={{0,4},{4,8},{8,12},{1,5},{5,9},{9,13},{2,6},{6,10},{10,14},{3,7},{... | collective-permute-start | bytes 1658888 | tf_op jit(solution)/shard_map/ppermute | solution.py:21
  17.7 2.0 copy.59
  19.8 6.0 %collective-permute-start.6 = (bf16[1,1,18,3,1]{3,2,4,1,0:T(8,128)(2,1)S(1)}, bf16[1,1,18,3,1]{3,2,4,1,0:T(8,128)(2,1)S(1)}, u32[]{:S(2)}, u32[]{:S(2)}) collective-permute-start(bf16[1,1,18,3,1]{3,2,4,1,0:T(8,128)(2,1)S(1)} %get-tuple-element.16), channel_id=1, source_target_pairs={{0,1},{1,2},{2,3},{4,5},{5,6},{6,7},{8,9},{9,10},{10,11},{12,13},{... | collective-permute-start | bytes 332 | tf_op jit(solution)/shard_map/ppermute | solution.py:21
  25.9 1.9 collective-permute-start.7
  27.8 5.5 %reshape.226 = bf16[480,16,72]{2,1,0:T(8,128)(2,1)} reshape(bf16[1,1,12,40,1152]{4,3,2,1,0:T(8,128)(2,1)} %slice.64) | data formatting | bytes 2211840 | tf_op jit(solution)/shard_map/reshape.3
  35.2 1.5 pad_maximum_fusion.3
  36.7 5.1 %collective-permute-start.2 = (bf16[2,1,18,3,1152]{4,2,3,1,0:T(8,128)(2,1)S(1)}, bf16[2,1,18,3,1152]{4,2,3,1,0:T(8,128)(2,1)S(1)}, u32[]{:S(2)}, u32[]{:S(2)}) collective-permute-start(bf16[2,1,18,3,1152]{4,2,3,1,0:T(8,128)(2,1)S(1)} %get-tuple-element.12), channel_id=1, source_target_pairs={{0,1},{1,2},{2,3},{4,5},{5,6},{6,7},{8,9},{9,10},{10,11},{12,13},{... | collective-permute-start | bytes 746504 | tf_op jit(solution)/shard_map/ppermute | solution.py:21
  41.9 1.9 collective-permute-start.3
  43.8 1.5 fusion.32
  45.9 5.9 %collective-permute-done.3 = bf16[2,1,18,3,1152]{4,2,3,1,0:T(8,128)(2,1)S(1)} collective-permute-done((bf16[2,1,18,3,1152]{4,2,3,1,0:T(8,128)(2,1)S(1)}, bf16[2,1,18,3,1152]{4,2,3,1,0:T(8,128)(2,1)S(1)}, u32[]{:S(2)}, u32[]{:S(2)}) %collective-permute-start.3) | collective-permute-done | bytes 248864 | tf_op jit(solution)/shard_map/ppermute | solution.py:22
  51.8 3.1 %pad_maximum_fusion = bf16[2,1,18,46,1152]{4,2,3,1,0:T(8,128)(2,1)S(1)} fusion(bf16[2,1,18,3,1152]{4,2,3,1,0:T(8,128)(2,1)S(1)} %collective-permute-done.3, bf16[2,1,3,40,1152]{4,2,3,1,0:T(4,128)(2,1)S(1)} %copy.39, bf16[2,1,12,40,1152]{4,2,3,1,0:T(8,128)(2,1)S(1)} %copy-done.1, bf16[2,1,3,40,1152]{4,2,3,1,0:T(4,128)(2,1)S(1)} %copy.38, ...), kind=kLoop, calls=%fused_computation.10 | loop fusion | flops 19077120 | bytes 7630848 | tf_op jit(solution)/shard_map/concatenate | solution.py:23
  54.9 1.9 fusion.61
  56.8 1.5 copy.41
  58.3 8.3 %reshape.225 = bf16[828,16,72]{2,1,0:T(8,128)(2,1)} reshape(bf16[1,1,18,46,1152]{4,3,2,1,0:T(8,128)(2,1)} %copy.41) | data formatting | bytes 3815424 | tf_op jit(solution)/shard_map/reshape.4
  66.6 3.2 %copy.40 = bf16[1,1,18,46,1152]{4,3,2,1,0:T(8,128)(2,1)} copy(bf16[1,1,18,46,1152]{4,2,3,1,0:T(8,128)(2,1)} %get-tuple-element.10) | data formatting | bytes 3815424 | tf_op jit(solution)/shard_map/slice | solution.py:69
  69.9 8.3 %reshape.224 = bf16[828,16,72]{2,1,0:T(8,128)(2,1)} reshape(bf16[1,1,18,46,1152]{4,3,2,1,0:T(8,128)(2,1)} %copy.40) | data formatting | bytes 3815424 | tf_op jit(solution)/shard_map/reshape.14
  78.2 18.5 %fusion.65 = (f32[16,480]{1,0:T(8,128)S(1)}, bf16[16,480,828]{1,2,0:T(8,128)(2,1)}) fusion(pred[480,828]{0,1:T(8,128)(4,1)S(1)} %fusion.32, bf16[828,16,72]{2,1,0:T(8,128)(2,1)} %reshape.225, bf16[480,16,72]{2,1,0:T(8,128)(2,1)} %reshape.226), kind=kOutput, calls=%fused_computation.89 | convolution fusion | flops 953856832 | bytes 16159872 | tf_op jit(solution)/shard_map/sub | solution.py:30
  96.7 9.1 %fusion.20 = bf16[1,480,16,72]{1,3,2,0:T(8,128)(2,1)S(1)} fusion(bf16[16,480,828]{1,2,0:T(8,128)(2,1)} %get-tuple-element.21, bf16[828,16,72]{2,1,0:T(8,128)(2,1)} %reshape.224, f32[480,16]{0,1:T(8,128)S(1)} %bitcast.66), kind=kOutput, calls=%fused_computation.24 | convolution fusion | flops 916807680 | bytes 15762432 | tf_op jit(solution)/shard_map/fhqk,fkhd->fqhd/dot_general | solution.py:87
  105.8 2.0 fusion.74
  108.2 9.8 %convolution_convert_fusion = bf16[480,3456]{1,0:T(8,128)(2,1)} fusion(bf16[1152,3456]{1,0:T(8,128)(2,1)} %param.11, f32[480,1152]{1,0:T(8,128)S(1)} %get-tuple-element.23, f32[1152]{0:T(1024)S(1)} %get-tuple-element.6, f32[1152]{0:T(1024)S(1)} %get-tuple-element.5, f32[480]{0:T(512)S(1)} %add_rsqrt_fusion, f32[480]{0:T(512)S(1)} %broadcast_multiply_fusion), kind=kOutput, calls=%fused_computation.9 | convolution fusion | flops 3826483200 | bytes 13505280 | tf_op jit(solution)/shard_map/dot_general | solution.py:103
  118.0 4.7 %reshape.228 = bf16[1,16,30,3456]{3,2,1,0:T(8,128)(2,1)} reshape(bf16[480,3456]{1,0:T(8,128)(2,1)} %convolution_convert_fusion) | data formatting | bytes 6635520 | tf_op jit(solution)/shard_map/reshape | solution.py:106
  122.7 83.5 %all_to_all.8 = bf16[1,16,30,3456]{3,2,0,1:T(8,128)(2,1)} all-to-all(bf16[1,16,30,3456]{3,2,0,1:T(8,128)(2,1)} %bitcast.59), channel_id=1, replica_groups=mesh['tm'=16,'row'=4,'col'=4] {'tm'}, dimensions={1} | all-to-all | bytes 6635520 | tf_op jit(solution)/shard_map/all_to_all | solution.py:109
  206.2 12.2 %reshape.234 = bf16[16,30,3,16,72]{4,3,2,1,0:T(8,128)(2,1)} reshape(bf16[1,16,30,3456]{3,2,0,1:T(8,128)(2,1)} %all_to_all.8) | data formatting | bytes 6635520 | tf_op jit(solution)/shard_map/reshape | solution.py:38
  218.4 3.8 %fusion.60 = (bf16[16,30,1,16,72]{4,3,2,1,0:T(8,128)(2,1)S(1)}, bf16[16,30,1,16,72]{4,3,2,1,0:T(8,128)(2,1)S(1)}, bf16[16,30,1,16,72]{4,3,2,1,0:T(8,128)(2,1)S(1)}) fusion(bf16[16,30,3,16,72]{4,3,2,1,0:T(8,128)(2,1)} %reshape.234), kind=kLoop, calls=%fused_computation.84 | loop fusion | bytes 6635520 | tf_op jit(solution)/shard_map/slice | solution.py:47
  222.3 1.9 multiply_reduce_fusion
  225.6 3.4 %fusion.9 = bf16[16,30,16,72]{3,0,2,1:T(8,128)(2,1)S(1)} fusion(f32[30,16,16,16]{2,3,1,0:T(8,128)S(1)} %get-tuple-element.25, bf16[16,30,1,16,72]{4,3,2,1,0:T(8,128)(2,1)S(1)} %get-tuple-element.7, f32[16,30,16]{0,2,1:T(8,128)S(1)} %bitcast.62, f32[30,16,16]{2,1,0:T(8,128)S(1)} %get-tuple-element.24), kind=kOutput, calls=%fused_computation.13 | convolution fusion | flops 19169280 | bytes 2764800 | tf_op jit(solution)/shard_map/phfg,gphd->fphd/dot_general | solution.py:46
  229.1 1.8 copy.54
  230.9 4.7 %reshape.233 = bf16[16,1,30,1152]{3,2,1,0:T(8,128)(2,1)} reshape(bf16[16,30,16,72]{3,2,1,0:T(8,128)(2,1)} %copy.54) | data formatting | bytes 2211840 | tf_op jit(solution)/shard_map/reshape | solution.py:50
  235.6 33.3 %all_to_all.9 = bf16[16,1,30,1152]{3,2,1,0:T(8,128)(2,1)} all-to-all(bf16[16,1,30,1152]{3,2,1,0:T(8,128)(2,1)} %reshape.233), channel_id=1, replica_groups=mesh['tm'=16,'row'=4,'col'=4] {'tm'}, dimensions={0} | all-to-all | bytes 2211840 | tf_op jit(solution)/shard_map/all_to_all | solution.py:107
  268.9 2.2 reshape.231
  (36 shorter events, 10.7 us)
Async XLA Ops:
  0.0 105.8 %copy-start = (bf16[1152,1152]{1,0:T(8,128)(2,1)S(1)}, bf16[1152,1152]{1,0:T(8,128)(2,1)}, u32[]{:S(2)}) copy-start(bf16[1152,1152]{1,0:T(8,128)(2,1)} %param.9) | copy-start | bytes 7962628
  0.9 18.8 %collective-permute-start.4 = (bf16[1,1,3,40,1]{3,2,4,1,0:T(4,128)(2,1)S(1)}, bf16[1,1,3,40,1]{3,2,4,1,0:T(4,128)(2,1)S(1)}, u32[]{:S(2)}, u32[]{:S(2)}) collective-permute-start(bf16[1,1,3,40,1]{3,2,4,1,0:T(4,128)(2,1)S(1)} %get-tuple-element.18), channel_id=1, source_target_pairs={{0,4},{4,8},{8,12},{1,5},{5,9},{9,13},{2,6},{6,10},{10,14},{3,7},{... | collective-permute-start | bytes 728 | tf_op jit(solution)/shard_map/ppermute | solution.py:21
  4.9 14.8 %collective-permute-start.5 = (bf16[1,1,3,40,1]{3,2,4,1,0:T(4,128)(2,1)S(1)}, bf16[1,1,3,40,1]{3,2,4,1,0:T(4,128)(2,1)S(1)}, u32[]{:S(2)}, u32[]{:S(2)}) collective-permute-start(bf16[1,1,3,40,1]{3,2,4,1,0:T(4,128)(2,1)S(1)} %get-tuple-element.19), channel_id=1, source_target_pairs={{4,0},{8,4},{12,8},{5,1},{9,5},{13,9},{6,2},{10,6},{14,10},{7,3},{... | collective-permute-start | bytes 728 | tf_op jit(solution)/shard_map/ppermute | solution.py:22
  8.5 7.2 %copy-start.2 = (bf16[3,1,12,40,1152]{4,3,2,1,0:T(8,128)(2,1)S(1)}, bf16[3,1,12,40,1152]{4,3,2,1,0:T(8,128)(2,1)}, u32[]{:S(2)}) copy-start(bf16[3,1,12,40,1152]{4,3,2,1,0:T(8,128)(2,1)} %param.7) | copy-start | bytes 9953284
  8.5 25.0 %collective-permute-start = (bf16[2,1,3,40,1152]{4,3,2,1,0:T(8,128)(2,1)}, bf16[2,1,3,40,1152]{4,3,2,1,0:T(8,128)(2,1)}, u32[]{:S(2)}, u32[]{:S(2)}) collective-permute-start(bf16[2,1,3,40,1152]{4,3,2,1,0:T(8,128)(2,1)} %get-tuple-element.14), channel_id=1, source_target_pairs={{0,4},{4,8},{8,12},{1,5},{5,9},{9,13},{2,6},{6,10},{10,14},{3,7},{... | collective-permute-start | bytes 1658888 | tf_op jit(solution)/shard_map/ppermute | solution.py:21
  13.5 21.3 %collective-permute-start.1 = (bf16[2,1,3,40,1152]{4,3,2,1,0:T(8,128)(2,1)}, bf16[2,1,3,40,1152]{4,3,2,1,0:T(8,128)(2,1)S(1)}, u32[]{:S(2)}, u32[]{:S(2)}) collective-permute-start(bf16[2,1,3,40,1152]{4,3,2,1,0:T(8,128)(2,1)} %get-tuple-element.15), channel_id=1, source_target_pairs={{4,0},{8,4},{12,8},{5,1},{9,5},{13,9},{6,2},{10,6},{14,10},{7,3},{... | collective-permute-start | bytes 1658888 | tf_op jit(solution)/shard_map/ppermute | solution.py:22
  15.7 2.0 slice-start
  19.8 13.5 %collective-permute-start.6 = (bf16[1,1,18,3,1]{3,2,4,1,0:T(8,128)(2,1)S(1)}, bf16[1,1,18,3,1]{3,2,4,1,0:T(8,128)(2,1)S(1)}, u32[]{:S(2)}, u32[]{:S(2)}) collective-permute-start(bf16[1,1,18,3,1]{3,2,4,1,0:T(8,128)(2,1)S(1)} %get-tuple-element.16), channel_id=1, source_target_pairs={{0,1},{1,2},{2,3},{4,5},{5,6},{6,7},{8,9},{9,10},{10,11},{12,13},{... | collective-permute-start | bytes 332 | tf_op jit(solution)/shard_map/ppermute | solution.py:21
  25.9 7.4 %collective-permute-start.7 = (bf16[1,1,18,3,1]{3,2,4,1,0:T(8,128)(2,1)S(1)}, bf16[1,1,18,3,1]{3,2,4,1,0:T(8,128)(2,1)S(1)}, u32[]{:S(2)}, u32[]{:S(2)}) collective-permute-start(bf16[1,1,18,3,1]{3,2,4,1,0:T(8,128)(2,1)S(1)} %get-tuple-element.17), channel_id=1, source_target_pairs={{1,0},{2,1},{3,2},{5,4},{6,5},{7,6},{9,8},{10,9},{11,10},{13,12},{... | collective-permute-start | bytes 332 | tf_op jit(solution)/shard_map/ppermute | solution.py:22
  35.2 16.6 %copy-start.1 = (bf16[2,1,12,40,1152]{4,2,3,1,0:T(8,128)(2,1)S(1)}, bf16[2,1,12,40,1152]{4,2,3,1,0:T(8,128)(2,1)}, u32[]{:S(2)}) copy-start(bf16[2,1,12,40,1152]{4,2,3,1,0:T(8,128)(2,1)} %copy.59) | copy-start | bytes 6635524
  36.7 9.2 %collective-permute-start.2 = (bf16[2,1,18,3,1152]{4,2,3,1,0:T(8,128)(2,1)S(1)}, bf16[2,1,18,3,1152]{4,2,3,1,0:T(8,128)(2,1)S(1)}, u32[]{:S(2)}, u32[]{:S(2)}) collective-permute-start(bf16[2,1,18,3,1152]{4,2,3,1,0:T(8,128)(2,1)S(1)} %get-tuple-element.12), channel_id=1, source_target_pairs={{0,1},{1,2},{2,3},{4,5},{5,6},{6,7},{8,9},{9,10},{10,11},{12,13},{... | collective-permute-start | bytes 746504 | tf_op jit(solution)/shard_map/ppermute | solution.py:21
  41.9 9.9 %collective-permute-start.3 = (bf16[2,1,18,3,1152]{4,2,3,1,0:T(8,128)(2,1)S(1)}, bf16[2,1,18,3,1152]{4,2,3,1,0:T(8,128)(2,1)S(1)}, u32[]{:S(2)}, u32[]{:S(2)}) collective-permute-start(bf16[2,1,18,3,1152]{4,2,3,1,0:T(8,128)(2,1)S(1)} %get-tuple-element.13), channel_id=1, source_target_pairs={{1,0},{2,1},{3,2},{5,4},{6,5},{7,6},{9,8},{10,9},{11,10},{13,12},{... | collective-permute-start | bytes 746504 | tf_op jit(solution)/shard_map/ppermute | solution.py:22
  96.7 9.1 %copy-start.3 = (bf16[1,12,40,1152]{3,2,1,0:T(8,128)(2,1)S(1)}, bf16[1,12,40,1152]{3,2,1,0:T(8,128)(2,1)}, u32[]{:S(2)}) copy-start(bf16[1,12,40,1152]{3,2,1,0:T(8,128)(2,1)} %param.6) | copy-start | bytes 3317764
where the time goes:
time: 272 us; the launch traced here: 271 us
  blocking collectives  117 us (43%)
  local copies, waits for them, and re-layouts  66.4 us (24%)
  matrix products  44.7 us (16%)
  starting transfers between devices  26.7 us (10%)
  other arithmetic  9.73 us (4%)
  waiting for transfers between devices  6.54 us (2%)
    all_to_all x1, blocking collectives, per_device(): lax.all_to_all(projected, 'tm', split_axis=1, concat_axis=0, tiled=True)  83.5 us
    all_to_all x1, blocking collectives, per_device(): lax.all_to_all(frame_attend(lax.all_to_all(projected, 'tm', split_axis=1,...  33.3 us
    another operation x3, local copies, waits for them, and re-layouts  22.2 us
    ppermute x4, starting transfers between devices, extended(): before = lax.ppermute(last, axis, up)  20.2 us
    sub x1, matrix products, softmax_parts(): weights_f = jnp.where(allowed, jnp.exp(masked - top_score), 0.0)  18.5 us
    reshape x1, local copies, waits for them, and re-layouts, frame_attend(): split_qkv = gathered.reshape(frames_all, items, 3, head_count, head_size)  12.2 us
    dot_general x1, matrix products, per_device(): jnp.dot(normed, w_temporal_qkv, preferred_element_type=jnp.float32)  9.82 us
    dot_general x1, matrix products, per_device(): jnp.einsum('fhqk,fkhd->fqhd', weights_b, values_pad, preferred_element_ty...  9.09 us
  transfers between devices with their start and end apart: 8, of which 2 were waited for; matrix products, arithmetic and copies ran while one was open for 5% of the time, Pallas kernels for 0%

commit v1 on v0

--- a/solution.py
+++ b/solution.py
@@ -100,18 +100,21 @@
     ).astype(jnp.bfloat16)
     tm_count = lax.axis_size("tm")
     part_tokens = tile_tokens // tm_count
-    projected = jnp.dot(normed, w_temporal_qkv, preferred_element_type=jnp.float32).astype(
-        jnp.bfloat16
+    exchanged = lax.all_to_all(
+        normed.reshape(frame_count, tm_count, part_tokens, width),
+        "tm",
+        split_axis=1,
+        concat_axis=0,
+        tiled=True,
     )
-    projected = projected.reshape(frame_count, tm_count, part_tokens, 3 * width)
+    projected = jnp.dot(
+        exchanged.reshape(tm_count * part_tokens, width),
+        w_temporal_qkv,
+        preferred_element_type=jnp.float32,
+    ).astype(jnp.bfloat16)
+    projected = projected.reshape(tm_count, frame_count, part_tokens, 3 * width)
     result = lax.all_to_all(
-        frame_attend(
-            lax.all_to_all(projected, "tm", split_axis=1, concat_axis=0, tiled=True), HEADS
-        ),
-        "tm",
-        split_axis=0,
-        concat_axis=1,
-        tiled=True,
+        frame_attend(projected, HEADS), "tm", split_axis=0, concat_axis=1, tiled=True
     )
     return result.reshape(frame_count, tile_rows, tile_cols, width)
 

time: 272 us -> 225 us (0.83)
  blocking collectives: 117 us -> 67.4 us
    all_to_all x2, blocking collectives: 117 us -> 67.4 us  [the longest x1 33.9 us: per_device(): lax.all_to_all(normed.reshape(frame_count, tm_count, part_tokens, width),...]
    another operation x3 -> x4, local copies, waits for them, and re-layouts: 22.2 us -> 35.1 us
    reshape x2, local copies, waits for them, and re-layouts: 16.9 us -> 4.42 us  [the longest x1 2.22 us: per_device(): normed.reshape(frame_count, tm_count, part_tokens, width)]
  transfers between devices with their start and end apart: 8 -> 8, of which waited for: 2 -> 2; matrix products, arithmetic and copies ran while one was open for 5% -> 7% of each run, Pallas kernels for 0% -> 0%
where the time goes in v1:
time: 225 us; the launch traced here: 224 us
  blocking collectives  67.4 us (30%)
  local copies, waits for them, and re-layouts  66.8 us (30%)
  matrix products  44.8 us (20%)
  starting transfers between devices  26.7 us (12%)
  other arithmetic  11.2 us (5%)
  waiting for transfers between devices  6.54 us (3%)
    all_to_all x1, blocking collectives, per_device(): lax.all_to_all(normed.reshape(frame_count, tm_count, part_tokens, width),...  33.9 us
    all_to_all x1, blocking collectives, per_device(): lax.all_to_all(frame_attend(projected, HEADS), 'tm', split_axis=0, concat...  33.5 us
    another operation x3, local copies, waits for them, and re-layouts  22.2 us
    ppermute x4, starting transfers between devices, extended(): before = lax.ppermute(last, axis, up)  20.2 us
    sub x1, matrix products, softmax_parts(): weights_f = jnp.where(allowed, jnp.exp(masked - top_score), 0.0)  18.5 us
    another operation x1, local copies, waits for them, and re-layouts, frame_attend(): split_qkv = gathered.reshape(frames_all, items, 3, head_count, head_size)  13 us
    dot_general x1, matrix products, per_device(): jnp.dot(exchanged.reshape(tm_count * part_tokens, width), w_temporal_qkv,...  9.94 us
    dot_general x1, matrix products, per_device(): jnp.einsum('fhqk,fkhd->fqhd', weights_b, values_pad, preferred_element_ty...  9.09 us
  transfers between devices with their start and end apart: 8, of which 2 were waited for; matrix products, arithmetic and copies ran while one was open for 7% of the time, Pallas kernels for 0%

profile of v1, /device:TPU:1, one launch (start us, length us, event | category | flops | bytes accessed | tf_op | source)
XLA Modules:
  0.0 223.6 jit_solution(13028056535932022726)
XLA Ops:
  0.9 4.0 %collective-permute-start.4 = (bf16[1,1,3,40,1]{3,2,4,1,0:T(4,128)(2,1)S(1)}, bf16[1,1,3,40,1]{3,2,4,1,0:T(4,128)(2,1)S(1)}, u32[]{:S(2)}, u32[]{:S(2)}) collective-permute-start(bf16[1,1,3,40,1]{3,2,4,1,0:T(4,128)(2,1)S(1)} %get-tuple-element.18), channel_id=1, source_target_pairs={{0,4},{4,8},{8,12},{1,5},{5,9},{9,13},{2,6},{6,10},{10,14},{3,7},{... | collective-permute-start | bytes 728 | tf_op jit(solution)/shard_map/ppermute | solution.py:21
  6.2 2.3 %fusion.58 = (bf16[2,1,3,40,1152]{4,3,2,1,0:T(8,128)(2,1)}, bf16[2,1,3,40,1152]{4,3,2,1,0:T(8,128)(2,1)}) fusion(bf16[3,1,12,40,1152]{4,3,2,1,0:T(8,128)(2,1)} %param.7), kind=kLoop, calls=%fused_computation.82 | loop fusion | bytes 2211840 | tf_op jit(solution)/shard_map/slice | solution.py:19
  8.5 5.0 %collective-permute-start = (bf16[2,1,3,40,1152]{4,3,2,1,0:T(8,128)(2,1)}, bf16[2,1,3,40,1152]{4,3,2,1,0:T(8,128)(2,1)}, u32[]{:S(2)}, u32[]{:S(2)}) collective-permute-start(bf16[2,1,3,40,1152]{4,3,2,1,0:T(8,128)(2,1)} %get-tuple-element.14), channel_id=1, source_target_pairs={{0,4},{4,8},{8,12},{1,5},{5,9},{9,13},{2,6},{6,10},{10,14},{3,7},{... | collective-permute-start | bytes 1658888 | tf_op jit(solution)/shard_map/ppermute | solution.py:21
  17.7 2.0 copy.57
  19.8 6.0 %collective-permute-start.6 = (bf16[1,1,18,3,1]{3,2,4,1,0:T(8,128)(2,1)S(1)}, bf16[1,1,18,3,1]{3,2,4,1,0:T(8,128)(2,1)S(1)}, u32[]{:S(2)}, u32[]{:S(2)}) collective-permute-start(bf16[1,1,18,3,1]{3,2,4,1,0:T(8,128)(2,1)S(1)} %get-tuple-element.16), channel_id=1, source_target_pairs={{0,1},{1,2},{2,3},{4,5},{5,6},{6,7},{8,9},{9,10},{10,11},{12,13},{... | collective-permute-start | bytes 332 | tf_op jit(solution)/shard_map/ppermute | solution.py:21
  25.9 1.9 collective-permute-start.7
  27.8 5.5 %reshape.226 = bf16[480,16,72]{2,1,0:T(8,128)(2,1)} reshape(bf16[1,1,12,40,1152]{4,3,2,1,0:T(8,128)(2,1)} %slice.64) | data formatting | bytes 2211840 | tf_op jit(solution)/shard_map/reshape.3
  35.2 1.5 pad_maximum_fusion.3
  36.7 5.1 %collective-permute-start.2 = (bf16[2,1,18,3,1152]{4,2,3,1,0:T(8,128)(2,1)S(1)}, bf16[2,1,18,3,1152]{4,2,3,1,0:T(8,128)(2,1)S(1)}, u32[]{:S(2)}, u32[]{:S(2)}) collective-permute-start(bf16[2,1,18,3,1152]{4,2,3,1,0:T(8,128)(2,1)S(1)} %get-tuple-element.12), channel_id=1, source_target_pairs={{0,1},{1,2},{2,3},{4,5},{5,6},{6,7},{8,9},{9,10},{10,11},{12,13},{... | collective-permute-start | bytes 746504 | tf_op jit(solution)/shard_map/ppermute | solution.py:21
  41.9 1.9 collective-permute-start.3
  45.9 5.9 %collective-permute-done.3 = bf16[2,1,18,3,1152]{4,2,3,1,0:T(8,128)(2,1)S(1)} collective-permute-done((bf16[2,1,18,3,1152]{4,2,3,1,0:T(8,128)(2,1)S(1)}, bf16[2,1,18,3,1152]{4,2,3,1,0:T(8,128)(2,1)S(1)}, u32[]{:S(2)}, u32[]{:S(2)}) %collective-permute-start.3) | collective-permute-done | bytes 248864 | tf_op jit(solution)/shard_map/ppermute | solution.py:22
  51.8 3.1 %pad_maximum_fusion = bf16[2,1,18,46,1152]{4,2,3,1,0:T(8,128)(2,1)S(1)} fusion(bf16[2,1,18,3,1152]{4,2,3,1,0:T(8,128)(2,1)S(1)} %collective-permute-done.3, bf16[2,1,3,40,1152]{4,2,3,1,0:T(4,128)(2,1)S(1)} %copy.40, bf16[2,1,12,40,1152]{4,2,3,1,0:T(8,128)(2,1)S(1)} %copy-done.1, bf16[2,1,3,40,1152]{4,2,3,1,0:T(4,128)(2,1)S(1)} %copy.39, ...), kind=kLoop, calls=%fused_computation.10 | loop fusion | flops 19077120 | bytes 7630848 | tf_op jit(solution)/shard_map/concatenate | solution.py:23
  54.9 1.9 fusion.57
  56.8 1.5 copy.42
  58.3 8.3 %reshape.225 = bf16[828,16,72]{2,1,0:T(8,128)(2,1)} reshape(bf16[1,1,18,46,1152]{4,3,2,1,0:T(8,128)(2,1)} %copy.42) | data formatting | bytes 3815424 | tf_op jit(solution)/shard_map/reshape.4
  66.6 3.2 %copy.41 = bf16[1,1,18,46,1152]{4,3,2,1,0:T(8,128)(2,1)} copy(bf16[1,1,18,46,1152]{4,2,3,1,0:T(8,128)(2,1)} %get-tuple-element.10) | data formatting | bytes 3815424 | tf_op jit(solution)/shard_map/slice | solution.py:69
  69.9 8.3 %reshape.224 = bf16[828,16,72]{2,1,0:T(8,128)(2,1)} reshape(bf16[1,1,18,46,1152]{4,3,2,1,0:T(8,128)(2,1)} %copy.41) | data formatting | bytes 3815424 | tf_op jit(solution)/shard_map/reshape.14
  78.2 18.5 %fusion.61 = (f32[16,480]{1,0:T(8,128)S(1)}, bf16[16,480,828]{1,2,0:T(8,128)(2,1)}) fusion(pred[480,828]{0,1:T(8,128)(4,1)S(1)} %fusion.32, bf16[828,16,72]{2,1,0:T(8,128)(2,1)} %reshape.225, bf16[480,16,72]{2,1,0:T(8,128)(2,1)} %reshape.226), kind=kOutput, calls=%fused_computation.85 | convolution fusion | flops 953856832 | bytes 16159872 | tf_op jit(solution)/shard_map/sub | solution.py:30
  96.7 9.1 %fusion.20 = bf16[1,480,16,72]{1,3,2,0:T(8,128)(2,1)S(1)} fusion(bf16[16,480,828]{1,2,0:T(8,128)(2,1)} %get-tuple-element.21, bf16[828,16,72]{2,1,0:T(8,128)(2,1)} %reshape.224, f32[480,16]{0,1:T(8,128)S(1)} %bitcast.67), kind=kOutput, calls=%fused_computation.24 | convolution fusion | flops 916807680 | bytes 15762432 | tf_op jit(solution)/shard_map/fhqk,fkhd->fqhd/dot_general | solution.py:87
  105.8 2.0 fusion.70
  109.6 2.2 reshape.228
  111.8 33.9 %all_to_all.8 = bf16[1,16,30,1152]{3,2,0,1:T(8,128)(2,1)} all-to-all(bf16[1,16,30,1152]{3,2,0,1:T(8,128)(2,1)} %bitcast.60), channel_id=1, replica_groups=mesh['tm'=16,'row'=4,'col'=4] {'tm'}, dimensions={1} | all-to-all | bytes 2211840 | tf_op jit(solution)/shard_map/all_to_all | solution.py:103
  145.7 2.2 reshape.229
  147.9 9.9 %convolution_convert_fusion = bf16[480,3456]{1,0:T(8,128)(2,1)} fusion(bf16[480,1152]{1,0:T(8,128)(2,1)} %reshape.229, bf16[1152,3456]{1,0:T(8,128)(2,1)} %param.11), kind=kOutput, calls=%fused_computation.9 | convolution fusion | flops 3823718400 | bytes 12386304 | tf_op jit(solution)/shard_map/dot_general | solution.py:110
  157.8 13.0 %reshape_reshape.3 = bf16[16,30,3,16,72]{4,3,2,1,0:T(8,128)(2,1)} reshape(bf16[480,3456]{1,0:T(8,128)(2,1)} %convolution_convert_fusion) | data formatting | bytes 6635520 | tf_op jit(solution)/shard_map/reshape;reshape | solution.py:38
  170.8 3.8 %fusion.56 = (bf16[16,30,1,16,72]{4,3,2,1,0:T(8,128)(2,1)S(1)}, bf16[16,30,1,16,72]{4,3,2,1,0:T(8,128)(2,1)S(1)}, bf16[16,30,1,16,72]{4,3,2,1,0:T(8,128)(2,1)S(1)}) fusion(bf16[16,30,3,16,72]{4,3,2,1,0:T(8,128)(2,1)} %reshape_reshape.3), kind=kLoop, calls=%fused_computation.80 | loop fusion | bytes 6635520 | tf_op jit(solution)/shard_map/slice | solution.py:47
  174.6 1.9 multiply_reduce_fusion
  178.0 3.4 %fusion.9 = bf16[16,30,16,72]{3,0,2,1:T(8,128)(2,1)S(1)} fusion(f32[30,16,16,16]{2,3,1,0:T(8,128)S(1)} %get-tuple-element.25, bf16[16,30,1,16,72]{4,3,2,1,0:T(8,128)(2,1)S(1)} %get-tuple-element.7, f32[16,30,16]{0,2,1:T(8,128)S(1)} %bitcast.63, f32[30,16,16]{2,1,0:T(8,128)S(1)} %get-tuple-element.24), kind=kOutput, calls=%fused_computation.13 | convolution fusion | flops 19169280 | bytes 2764800 | tf_op jit(solution)/shard_map/phfg,gphd->fphd/dot_general | solution.py:46
  181.4 1.8 copy.54
  183.2 4.7 %reshape.233 = bf16[16,1,30,1152]{3,2,1,0:T(8,128)(2,1)} reshape(bf16[16,30,16,72]{3,2,1,0:T(8,128)(2,1)} %copy.54) | data formatting | bytes 2211840 | tf_op jit(solution)/shard_map/reshape | solution.py:50
  187.9 33.5 %all_to_all.9 = bf16[16,1,30,1152]{3,2,1,0:T(8,128)(2,1)} all-to-all(bf16[16,1,30,1152]{3,2,1,0:T(8,128)(2,1)} %reshape.233), channel_id=1, replica_groups=mesh['tm'=16,'row'=4,'col'=4] {'tm'}, dimensions={0} | all-to-all | bytes 2211840 | tf_op jit(solution)/shard_map/all_to_all | solution.py:116
  221.4 2.2 reshape.231
  (38 shorter events, 13.6 us)
Async XLA Ops:
  0.0 105.8 %copy-start = (bf16[1152,1152]{1,0:T(8,128)(2,1)S(1)}, bf16[1152,1152]{1,0:T(8,128)(2,1)}, u32[]{:S(2)}) copy-start(bf16[1152,1152]{1,0:T(8,128)(2,1)} %param.9) | copy-start | bytes 7962628
  0.9 18.8 %collective-permute-start.4 = (bf16[1,1,3,40,1]{3,2,4,1,0:T(4,128)(2,1)S(1)}, bf16[1,1,3,40,1]{3,2,4,1,0:T(4,128)(2,1)S(1)}, u32[]{:S(2)}, u32[]{:S(2)}) collective-permute-start(bf16[1,1,3,40,1]{3,2,4,1,0:T(4,128)(2,1)S(1)} %get-tuple-element.18), channel_id=1, source_target_pairs={{0,4},{4,8},{8,12},{1,5},{5,9},{9,13},{2,6},{6,10},{10,14},{3,7},{... | collective-permute-start | bytes 728 | tf_op jit(solution)/shard_map/ppermute | solution.py:21
  4.9 14.8 %collective-permute-start.5 = (bf16[1,1,3,40,1]{3,2,4,1,0:T(4,128)(2,1)S(1)}, bf16[1,1,3,40,1]{3,2,4,1,0:T(4,128)(2,1)S(1)}, u32[]{:S(2)}, u32[]{:S(2)}) collective-permute-start(bf16[1,1,3,40,1]{3,2,4,1,0:T(4,128)(2,1)S(1)} %get-tuple-element.19), channel_id=1, source_target_pairs={{4,0},{8,4},{12,8},{5,1},{9,5},{13,9},{6,2},{10,6},{14,10},{7,3},{... | collective-permute-start | bytes 728 | tf_op jit(solution)/shard_map/ppermute | solution.py:22
  8.5 7.2 %copy-start.2 = (bf16[3,1,12,40,1152]{4,3,2,1,0:T(8,128)(2,1)S(1)}, bf16[3,1,12,40,1152]{4,3,2,1,0:T(8,128)(2,1)}, u32[]{:S(2)}) copy-start(bf16[3,1,12,40,1152]{4,3,2,1,0:T(8,128)(2,1)} %param.7) | copy-start | bytes 9953284
  8.5 25.0 %collective-permute-start = (bf16[2,1,3,40,1152]{4,3,2,1,0:T(8,128)(2,1)}, bf16[2,1,3,40,1152]{4,3,2,1,0:T(8,128)(2,1)}, u32[]{:S(2)}, u32[]{:S(2)}) collective-permute-start(bf16[2,1,3,40,1152]{4,3,2,1,0:T(8,128)(2,1)} %get-tuple-element.14), channel_id=1, source_target_pairs={{0,4},{4,8},{8,12},{1,5},{5,9},{9,13},{2,6},{6,10},{10,14},{3,7},{... | collective-permute-start | bytes 1658888 | tf_op jit(solution)/shard_map/ppermute | solution.py:21
  13.5 21.3 %collective-permute-start.1 = (bf16[2,1,3,40,1152]{4,3,2,1,0:T(8,128)(2,1)}, bf16[2,1,3,40,1152]{4,3,2,1,0:T(8,128)(2,1)S(1)}, u32[]{:S(2)}, u32[]{:S(2)}) collective-permute-start(bf16[2,1,3,40,1152]{4,3,2,1,0:T(8,128)(2,1)} %get-tuple-element.15), channel_id=1, source_target_pairs={{4,0},{8,4},{12,8},{5,1},{9,5},{13,9},{6,2},{10,6},{14,10},{7,3},{... | collective-permute-start | bytes 1658888 | tf_op jit(solution)/shard_map/ppermute | solution.py:22
  15.7 2.0 slice-start
  19.8 13.5 %collective-permute-start.6 = (bf16[1,1,18,3,1]{3,2,4,1,0:T(8,128)(2,1)S(1)}, bf16[1,1,18,3,1]{3,2,4,1,0:T(8,128)(2,1)S(1)}, u32[]{:S(2)}, u32[]{:S(2)}) collective-permute-start(bf16[1,1,18,3,1]{3,2,4,1,0:T(8,128)(2,1)S(1)} %get-tuple-element.16), channel_id=1, source_target_pairs={{0,1},{1,2},{2,3},{4,5},{5,6},{6,7},{8,9},{9,10},{10,11},{12,13},{... | collective-permute-start | bytes 332 | tf_op jit(solution)/shard_map/ppermute | solution.py:21
  25.9 7.4 %collective-permute-start.7 = (bf16[1,1,18,3,1]{3,2,4,1,0:T(8,128)(2,1)S(1)}, bf16[1,1,18,3,1]{3,2,4,1,0:T(8,128)(2,1)S(1)}, u32[]{:S(2)}, u32[]{:S(2)}) collective-permute-start(bf16[1,1,18,3,1]{3,2,4,1,0:T(8,128)(2,1)S(1)} %get-tuple-element.17), channel_id=1, source_target_pairs={{1,0},{2,1},{3,2},{5,4},{6,5},{7,6},{9,8},{10,9},{11,10},{13,12},{... | collective-permute-start | bytes 332 | tf_op jit(solution)/shard_map/ppermute | solution.py:22
  35.2 16.6 %copy-start.1 = (bf16[2,1,12,40,1152]{4,2,3,1,0:T(8,128)(2,1)S(1)}, bf16[2,1,12,40,1152]{4,2,3,1,0:T(8,128)(2,1)}, u32[]{:S(2)}) copy-start(bf16[2,1,12,40,1152]{4,2,3,1,0:T(8,128)(2,1)} %copy.57) | copy-start | bytes 6635524
  36.7 9.2 %collective-permute-start.2 = (bf16[2,1,18,3,1152]{4,2,3,1,0:T(8,128)(2,1)S(1)}, bf16[2,1,18,3,1152]{4,2,3,1,0:T(8,128)(2,1)S(1)}, u32[]{:S(2)}, u32[]{:S(2)}) collective-permute-start(bf16[2,1,18,3,1152]{4,2,3,1,0:T(8,128)(2,1)S(1)} %get-tuple-element.12), channel_id=1, source_target_pairs={{0,1},{1,2},{2,3},{4,5},{5,6},{6,7},{8,9},{9,10},{10,11},{12,13},{... | collective-permute-start | bytes 746504 | tf_op jit(solution)/shard_map/ppermute | solution.py:21
  41.9 9.9 %collective-permute-start.3 = (bf16[2,1,18,3,1152]{4,2,3,1,0:T(8,128)(2,1)S(1)}, bf16[2,1,18,3,1152]{4,2,3,1,0:T(8,128)(2,1)S(1)}, u32[]{:S(2)}, u32[]{:S(2)}) collective-permute-start(bf16[2,1,18,3,1152]{4,2,3,1,0:T(8,128)(2,1)S(1)} %get-tuple-element.13), channel_id=1, source_target_pairs={{1,0},{2,1},{3,2},{5,4},{6,5},{7,6},{9,8},{10,9},{11,10},{13,12},{... | collective-permute-start | bytes 746504 | tf_op jit(solution)/shard_map/ppermute | solution.py:22
  96.7 9.1 %copy-start.3 = (bf16[1,12,40,1152]{3,2,1,0:T(8,128)(2,1)S(1)}, bf16[1,12,40,1152]{3,2,1,0:T(8,128)(2,1)}, u32[]{:S(2)}) copy-start(bf16[1,12,40,1152]{3,2,1,0:T(8,128)(2,1)} %param.6) | copy-start | bytes 3317764

commit v2 on v0

v2 whole, which is shorter than its diff:
```python
import jax
import jax.numpy as jnp
from jax import lax
from jax.experimental import pallas as pl
from jax.experimental.pallas import tpu as pltpu
from jax.sharding import PartitionSpec as P

HEADS = 16
RADIUS = 3
NEG_FILL = -1e30
EPSILON = 1e-06
LOG2E = 1.4426950408889634
LANES = 128
UNIT = 8
MESH = pl.DeviceIdType.MESH


def head_windows(width, heads):
    size = width // heads
    last = width // LANES - 2
    found = {}
    for head in range(heads):
        tile = min(head * size // LANES, last)
        if (tile - 1) in found and (head + 1) * size <= (tile + 1) * LANES:
            tile = tile - 1
        found.setdefault(tile, []).append(head)
    return sorted(found.items())


def attend(query, key, value, bias, heads, tile, size, out_ref):
    factor = size ** (-0.5) * LOG2E
    lane = lax.broadcasted_iota(jnp.int32, (1, 2 * LANES), 1) + tile * LANES
    place = slice(tile * LANES, (tile + 2) * LANES)
    current = out_ref[:, place]
    for head in heads:
        inside = (lane >= head * size) & (lane < (head + 1) * size)
        chosen = query * jnp.where(inside, 1.0, 0.0).astype(jnp.bfloat16)
        scores = lax.dot_general(
            chosen, key, (((1,), (1,)), ((), ())), preferred_element_type=jnp.float32
        )
        scores = scores + bias[...]
        top = jnp.max(scores, -1, keepdims=True)
        weights = jnp.exp2((scores - top) * factor)
        total = jnp.sum(weights, -1, keepdims=True)
        mixed = jnp.dot(
            weights.astype(jnp.bfloat16), value, preferred_element_type=jnp.float32
        )
        current = jnp.where(inside, mixed * (1.0 / total), current)
    out_ref[:, place] = current


def block_kernel(
    qkv, flags, resid, w_out, modulation, w_qkv,
    out,
    kb, vb, qb, rb, wo, mo, wq, hb, sbias, swin, ns, nr, tq, tb, tbias, ts,
    load_sem, col_send, col_recv, row_send, row_recv, cor_send, cor_recv,
    p1_send, p1_recv, p2_send, p2_recv, own_sem,
):
    me, row, col = lax.axis_index("tm"), lax.axis_index("row"), lax.axis_index("col")
    tm_count, row_count, col_count = (lax.axis_size(a) for a in ("tm", "row", "col"))
    _, tile_rows, tile_cols, width = qkv.shape
    size = width // HEADS
    windows = head_windows(width, HEADS)
    blocks = ns.shape[0] // (tm_count - 1)
    units = tm_count - 1
    block_rows = tile_rows // blocks
    rows_q = block_rows * tile_cols
    span = block_rows + 2 * RADIUS
    wide = tile_cols + 2 * UNIT
    keys = span * wide
    low, high = tile_rows, tile_rows + RADIUS
    own_rows = pl.ds(RADIUS, tile_rows)

    loads = [
        pltpu.make_async_copy(qkv.at[1], kb.at[own_rows, pl.ds(0, tile_cols), pl.ds(0, width)], load_sem.at[0]),
        pltpu.make_async_copy(flags, kb.at[own_rows, pl.ds(0, tile_cols), pl.ds(width, LANES)], load_sem.at[1]),
        pltpu.make_async_copy(qkv.at[0], qb, load_sem.at[2]),
        pltpu.make_async_copy(qkv.at[2], vb.at[own_rows, pl.ds(0, tile_cols)], load_sem.at[3]),
        pltpu.make_async_copy(w_out, wo, load_sem.at[4]),
        pltpu.make_async_copy(resid, rb, load_sem.at[5]),
        pltpu.make_async_copy(modulation, mo, load_sem.at[6]),
        pltpu.make_async_copy(w_qkv, wq, load_sem.at[7]),
    ]
    for load in loads:
        load.start()

    barrier = pltpu.get_barrier_semaphore()

    def greet(step, carry):
        pl.semaphore_signal(barrier, inc=1, device_id={"tm": lax.rem(me + step, tm_count)}, device_id_type=MESH)
        return carry

    lax.fori_loop(1, tm_count, greet, 0)
    for step in (1, row_count - 1):
        pl.semaphore_signal(barrier, inc=1, device_id={"row": lax.rem(row + step, row_count)}, device_id_type=MESH)
    for step in (1, col_count - 1):
        pl.semaphore_signal(barrier, inc=1, device_id={"col": lax.rem(col + step, col_count)}, device_id_type=MESH)

    def clear(rows, cols):
        for buffer in (kb, vb):
            view = buffer.at[rows, cols]
            view[...] = jnp.zeros(view.shape, view.dtype)

    everything = pl.ds(0, tile_rows + 2 * RADIUS)
    pl.when(row == 0)(lambda: clear(pl.ds(0, RADIUS), pl.ds(0, wide)))
    pl.when(row == row_count - 1)(lambda: clear(pl.ds(low + RADIUS, RADIUS), pl.ds(0, wide)))
    pl.when(col == 0)(lambda: clear(everything, pl.ds(tile_cols, UNIT)))
    pl.when(col == col_count - 1)(lambda: clear(everything, pl.ds(tile_cols + UNIT, UNIT)))
    hb[...] = jnp.zeros_like(hb)
    tb[...] = jnp.zeros_like(tb)

    shape = (rows_q, keys)
    q_at = lax.broadcasted_iota(jnp.int32, shape, 0)
    k_at = lax.broadcasted_iota(jnp.int32, shape, 1)
    q_row = sum((q_at >= tile_cols * i).astype(jnp.int32) for i in range(1, block_rows))
    k_row = sum((k_at >= wide * i).astype(jnp.int32) for i in range(1, span))
    q_col = q_at - q_row * tile_cols
    k_col = k_at - k_row * wide
    k_col = jnp.where(
        k_col < tile_cols, k_col, jnp.where(k_col < tile_cols + UNIT, k_col - tile_cols - UNIT, k_col - UNIT)
    )
    row_gap, col_gap = k_row - q_row - RADIUS, k_col - q_col
    near = (jnp.abs(row_gap) <= RADIUS) & (jnp.abs(col_gap) <= RADIUS)
    itself = (row_gap == 0) & (col_gap == 0)
    swin[...] = jnp.where(near, 1.0, 0.0) + jnp.where(itself, 1.0, 0.0)
    t_shape = tbias.shape
    same = (
        lax.broadcasted_iota(jnp.int32, t_shape, 0) - lax.broadcasted_iota(jnp.int32, t_shape, 1)
    ) & (UNIT - 1)
    tbias[...] = jnp.where(same == 0, 0.0, NEG_FILL)

    pl.semaphore_wait(barrier, tm_count - 1 + 4)

    def halo(source_rows, source_cols, target_rows, target_cols, sends, recvs, target):
        copies = []
        for index, (array, buffer, lanes) in enumerate(
            ((qkv.at[1], kb, (0, width)), (flags, kb, (width, LANES)), (qkv.at[2], vb, (0, width)))
        ):
            copies.append(
                pltpu.make_async_remote_copy(
                    src_ref=array.at[source_rows, source_cols],
                    dst_ref=buffer.at[target_rows, target_cols, pl.ds(*lanes)],
                    send_sem=sends.at[index],
                    recv_sem=recvs.at[index],
                    device_id=target,
                    device_id_type=MESH,
                )
            )
        return copies

    def relay(source_cols, target_cols, rows, sends, recvs, target):
        return [
            pltpu.make_async_remote_copy(
                src_ref=buffer.at[rows, source_cols],
                dst_ref=buffer.at[rows, target_cols],
                send_sem=sends.at[index],
                recv_sem=recvs.at[index],
                device_id=target,
                device_id_type=MESH,
            )
            for index, buffer in enumerate((kb, vb))
        ]

    right = {"col": lax.rem(col + 1, col_count)}
    left = {"col": lax.rem(col + col_count - 1, col_count)}
    down = {"row": lax.rem(row + 1, row_count)}
    up = {"row": lax.rem(row + row_count - 1, row_count)}
    has = {
        "right": col < col_count - 1, "left": col > 0, "down": row < row_count - 1, "up": row > 0,
    }
    first_cols, last_cols = pl.ds(0, UNIT), pl.ds(tile_cols - UNIT, UNIT)
    left_strip, right_strip = pl.ds(tile_cols, UNIT), pl.ds(tile_cols + UNIT, UNIT)
    all_rows, all_cols = pl.ds(0, tile_rows), pl.ds(0, tile_cols)
    top_halo, bottom_halo = pl.ds(0, RADIUS), pl.ds(low + RADIUS, RADIUS)
    to_right = halo(all_rows, last_cols, own_rows, left_strip, col_send.at[0], col_recv.at[0], right)
    to_left = halo(all_rows, first_cols, own_rows, right_strip, col_send.at[1], col_recv.at[1], left)
    to_down = halo(pl.ds(tile_rows - RADIUS, RADIUS), all_cols, top_halo, all_cols, row_send.at[0], row_recv.at[0], down)
    to_up = halo(pl.ds(0, RADIUS), all_cols, bottom_halo, all_cols, row_send.at[1], row_recv.at[1], up)

    def start(copies):
        for copy in copies:
            copy.start()

    def got(copies):
        for copy in copies:
            copy.wait_recv()

    def sent(copies):
        for copy in copies:
            copy.wait_send()

    pl.when(has["right"])(lambda: start(to_right))
    pl.when(has["left"])(lambda: start(to_left))
    pl.when(has["down"])(lambda: start(to_down))
    pl.when(has["up"])(lambda: start(to_up))

    corners = []
    for index, (rows, row_side) in enumerate(((top_halo, "up"), (bottom_halo, "down"))):
        corners.append(
            (relay(last_cols, left_strip, rows, cor_send.at[index, 0], cor_recv.at[index, 0], right),
             has[row_side] & has["right"], has[row_side] & has["left"])
        )
        corners.append(
            (relay(first_cols, right_strip, rows, cor_send.at[index, 1], cor_recv.at[index, 1], left),
             has[row_side] & has["left"], has[row_side] & has["right"])
        )

    for load in loads[:4]:
        load.wait()
    pl.when(has["left"])(lambda: got(to_right))
    pl.when(has["right"])(lambda: got(to_left))

    def unit_of(block, device):
        return lax.rem(device - 4 * block + 4 * tm_count, tm_count)

    def first_copy(block, owner):
        return pltpu.make_async_remote_copy(
            src_ref=ns.at[block * units + unit_of(block, owner)],
            dst_ref=nr.at[block, me],
            send_sem=p1_send.at[block],
            recv_sem=p1_recv.at[block],
            device_id={"tm": owner},
            device_id_type=MESH,
        )

    def second_copy(block, unit, frame):
        return pltpu.make_async_remote_copy(
            src_ref=ts.at[block, frame],
            dst_ref=out.at[block * units + unit],
            send_sem=p2_send.at[block],
            recv_sem=p2_recv.at[block],
            device_id={"tm": frame},
            device_id_type=MESH,
        )

    def spatial(step, carry):
        block = lax.rem(step + 1, blocks)

        @pl.when(step == 1)
        def _():
            pl.when(has["up"])(lambda: got(to_down))
            pl.when(has["down"])(lambda: got(to_up))
            for copies, sends, _ in corners:
                pl.when(sends)(lambda copies=copies: start(copies))

        @pl.when(step == 2)
        def _():
            for copies, _, receives in corners:
                pl.when(receives)(lambda copies=copies: got(copies))

        first = block * block_rows
        lane = lax.broadcasted_iota(jnp.int32, (UNIT, LANES), 1)
        pick = jnp.where(lane == 0, 1.0, 0.0).astype(jnp.bfloat16)
        live = kb[pl.ds(first, span), :, width : width + LANES].reshape(keys, LANES)
        keep = lax.dot_general(pick, live, (((1,), (1,)), ((), ())), preferred_element_type=jnp.float32)
        sbias[...] = jnp.where(swin[...] + keep[0:1] > 1.5, 0.0, NEG_FILL)
        for tile, heads in windows:
            place = slice(tile * LANES, (tile + 2) * LANES)
            query = qb[pl.ds(first, block_rows), :, place].reshape(rows_q, 2 * LANES)
            key = kb[pl.ds(first, span), :, place].reshape(keys, 2 * LANES)
            value = vb[pl.ds(first, span), :, place].reshape(keys, 2 * LANES)
            attend(query, key, value, sbias, heads, tile, size, hb)

        @pl.when(step == 0)
        def _():
            for load in loads[4:7]:
                load.wait()

        stream = rb[pl.ds(first, block_rows)].reshape(rows_q, width).astype(jnp.float32) + jnp.dot(
            hb[...].astype(jnp.bfloat16), wo[...], preferred_element_type=jnp.float32
        )
        average = jnp.mean(stream, -1, keepdims=True)
        centered = stream - average
        variance = jnp.mean(centered * centered, -1, keepdims=True)
        normed = centered * lax.rsqrt(variance + EPSILON) * (1.0 + mo[1:2]) + mo[0:1]
        ns[pl.ds(block * units, units)] = normed.astype(jnp.bfloat16).reshape(units, UNIT, width)
        mine = unit_of(block, me)

        @pl.when(mine < units)
        def _():
            nr[block, me] = ns[block * units + mine]

        def send(offset, carry):
            owner = lax.rem(me + offset, tm_count)

            @pl.when(unit_of(block, owner) < units)
            def _():
                first_copy(block, owner).start()

            return carry

        lax.fori_loop(1, tm_count, send, 0)
        return carry

    lax.fori_loop(0, blocks, spatial, 0)
    loads[7].wait()

    def temporal(step, carry):
        block = lax.rem(step + 1, blocks)
        mine = unit_of(block, me)

        @pl.when(mine < units)
        def _():
            arrived = nr.at[block, pl.ds(0, units)]
            pltpu.make_async_copy(arrived, arrived, p1_recv.at[block]).wait()
            rows = nr[block].reshape(tm_count * UNIT, width)
            for part in range(9):
                place = slice(part * 3 * LANES, (part + 1) * 3 * LANES)
                tq[:, place] = jnp.dot(
                    rows, wq[:, place], preferred_element_type=jnp.float32
                ).astype(jnp.bfloat16)
            for tile, heads in windows:
                place = [slice(i * width + tile * LANES, i * width + (tile + 2) * LANES) for i in range(3)]
                attend(tq[:, place[0]], tq[:, place[1]], tq[:, place[2]], tbias, heads, tile, size, tb)
            ts[block] = tb[...].astype(jnp.bfloat16).reshape(tm_count, UNIT, width)
            pltpu.make_async_copy(ts.at[block, me], out.at[block * units + mine], own_sem.at[block]).start()

            def send(offset, carry):
                second_copy(block, mine, lax.rem(me + offset, tm_count)).start()
                return carry

            lax.fori_loop(1, tm_count, send, 0)

        return carry

    lax.fori_loop(0, blocks, temporal, 0)

    pl.when(has["right"])(lambda: sent(to_right))
    pl.when(has["left"])(lambda: sent(to_left))
    pl.when(has["down"])(lambda: sent(to_down))
    pl.when(has["up"])(lambda: sent(to_up))
    for copies, sends, _ in corners:
        pl.when(sends)(lambda copies=copies: sent(copies))

    def finish(block, carry):
        mine = unit_of(block, me)

        @pl.when(mine < units)
        def _():
            part, whole = pl.ds(0, units - 1), pl.ds(0, units)
            pltpu.make_async_copy(ns.at[part], ns.at[part], p1_send.at[block]).wait()
            pltpu.make_async_copy(ts.at[block, whole], ts.at[block, whole], p2_send.at[block]).wait()
            pltpu.make_async_copy(out.at[part], out.at[part], p2_recv.at[block]).wait()
            pltpu.make_async_copy(ts.at[block, me], out.at[block * units + mine], own_sem.at[block]).wait()

        @pl.when(mine >= units)
        def _():
            whole = pl.ds(0, units)
            pltpu.make_async_copy(ns.at[whole], ns.at[whole], p1_send.at[block]).wait()
            pltpu.make_async_copy(out.at[whole], out.at[whole], p2_recv.at[block]).wait()

        return carry

    lax.fori_loop(0, blocks, finish, 0)


def per_device(resid, spatial_qkv, key_keep, w_spatial_out, modulation, w_temporal_qkv):
    frame_count, tile_rows, tile_cols, width = resid.shape
    tm_count = lax.axis_size("tm")
    units = tile_rows * tile_cols // UNIT
    blocks = units // (tm_count - 1)
    block_rows = tile_rows // blocks
    rows_q = block_rows * tile_cols
    wide = tile_cols + 2 * UNIT
    pad_rows = tile_rows + 2 * RADIUS
    keys = (block_rows + 2 * RADIUS) * wide
    flags = jnp.broadcast_to(
        key_keep[0].astype(jnp.bfloat16)[..., None], (tile_rows, tile_cols, LANES)
    )
    bf16, f32 = jnp.bfloat16, jnp.float32
    dma = pltpu.SemaphoreType.DMA
    anywhere = pl.BlockSpec(memory_space=pl.ANY)
    result = pl.pallas_call(
        block_kernel,
        out_shape=jax.ShapeDtypeStruct((units, UNIT, width), bf16),
        in_specs=[anywhere] * 6,
        out_specs=anywhere,
        scratch_shapes=[
            pltpu.VMEM((pad_rows, wide, width + LANES), bf16),
            pltpu.VMEM((pad_rows, wide, width), bf16),
            pltpu.VMEM((tile_rows, tile_cols, width), bf16),
            pltpu.VMEM((tile_rows, tile_cols, width), bf16),
            pltpu.VMEM((width, width), bf16),
            pltpu.VMEM((2, width), f32),
            pltpu.VMEM((width, 3 * width), bf16),
            pltpu.VMEM((rows_q, width), f32),
            pltpu.VMEM((rows_q, keys), f32),
            pltpu.VMEM((rows_q, keys), f32),
            pltpu.VMEM((units, UNIT, width), bf16),
            pltpu.VMEM((blocks, tm_count, UNIT, width), bf16),
            pltpu.VMEM((tm_count * UNIT, 3 * width), bf16),
            pltpu.VMEM((tm_count * UNIT, width), f32),
            pltpu.VMEM((tm_count * UNIT, tm_count * UNIT), f32),
            pltpu.VMEM((blocks, tm_count, UNIT, width), bf16),
            dma((8,)),
            dma((2, 3)), dma((2, 3)), dma((2, 3)), dma((2, 3)), dma((2, 2, 2)), dma((2, 2, 2)),
            dma((blocks,)), dma((blocks,)), dma((blocks,)), dma((blocks,)), dma((blocks,)),
        ],
        compiler_params=pltpu.CompilerParams(
            collective_id=0, has_side_effects=True, vmem_limit_bytes=60 * 1024 * 1024
        ),
    )(
        spatial_qkv.reshape(3, tile_rows, tile_cols, width),
        flags,
        resid.reshape(tile_rows, tile_cols, width),
        w_spatial_out,
        modulation,
        w_temporal_qkv,
    )
    return result.reshape(frame_count, tile_rows, tile_cols, width)


def solution(mesh):
    return jax.shard_map(
        per_device,
        mesh=mesh,
        in_specs=(
            P("tm", "row", "col", None),
            P(None, "tm", "row", "col", None),
            P("tm", "row", "col"),
            P(),
            P(),
            P(),
        ),
        out_specs=P("tm", "row", "col", None),
        check_vma=False,
    )
```

time: 272 us -> 81.6 us (0.30)
  blocking collectives: 117 us -> 0 us
  Pallas kernels: 0 us -> 77.6 us
  local copies, waits for them, and re-layouts: 66.4 us -> 3.11 us
  matrix products: 44.7 us -> 0 us
  starting transfers between devices: 26.7 us -> 0 us
  other arithmetic: 9.73 us -> 0.7 us
  waiting for transfers between devices: 6.54 us -> 0 us
    all_to_all x2 -> x0, blocking collectives: 117 us -> none  [the longest x1 83.5 us: per_device(): lax.all_to_all(projected, 'tm', split_axis=1, concat_axis=0, tiled=True)]
    pallas_call x0 -> x1, Pallas kernels: none -> 77.6 us  [per_device(): pl.pallas_call(block_kernel, out_shape=jax.ShapeDtypeStruct((units, UNIT,...]
    ppermute x8 -> x0, starting transfers between devices: 26.7 us -> none  [the longest x4 20.2 us: extended(): before = lax.ppermute(last, axis, up)]
    dot_general x5 -> x0, matrix products: 26.3 us -> none  [the longest x1 9.82 us: per_device(): jnp.dot(normed, w_temporal_qkv, preferred_element_type=jnp.float32)]
    reshape x5 -> x0, local copies, waits for them, and re-layouts: 25.6 us -> none  [the longest x1 12.2 us: frame_attend(): split_qkv = gathered.reshape(frames_all, items, 3, head_count, head_size)]
    another operation x3 -> x0, local copies, waits for them, and re-layouts: 22.2 us -> none
    sub x1 -> x0, matrix products: 18.5 us -> none  [softmax_parts(): weights_f = jnp.where(allowed, jnp.exp(masked - top_score), 0.0)]
    slice x10 -> x0, local copies, waits for them, and re-layouts: 14.8 us -> none  [the longest x2 5.09 us: per_device(): padded_pair[1].reshape(frame_count, key_count, HEADS, head_size)]
  transfers between devices with their start and end apart: 8 -> 0, of which waited for: 2 -> 0; matrix products, arithmetic and copies ran while one was open for 5% -> 0% of each run, Pallas kernels for 0% -> 0%
where the time goes in v2:
time: 81.6 us; the launch traced here: 81.4 us
  Pallas kernels  77.6 us (95%)
  local copies, waits for them, and re-layouts  3.11 us (4%)
    pallas_call x1, Pallas kernels, per_device(): pl.pallas_call(block_kernel, out_shape=jax.ShapeDtypeStruct((units, UNIT,...  77.6 us
    unnamed x2, local copies, waits for them, and re-layouts  2.32 us

profile of v2, /device:TPU:1, one launch (start us, length us, event | category | flops | bytes accessed | tf_op | source)
XLA Modules:
  0.0 81.4 jit_solution(6817800952360337308)
XLA Ops:
  0.0 0.7 convert_element_type.10
  0.7 0.8 broadcast_in_dim.2.flags
  1.5 77.6 %shard_map.64 = bf16[60,8,1152]{2,1,0:T(8,128)(2,1)} custom-call(bf16[3,12,40,1152]{3,2,1,0:T(8,128)(2,1)} %bitcast.7, bf16[12,40,128]{2,1,0:T(8,128)(2,1)} %broadcast_in_dim.2.flags, bf16[12,40,1152]{2,1,0:T(8,128)(2,1)} %bitcast.8, bf16[1152,1152]{1,0:T(8,128)(2,1)} %w_out.1, f32[2,1152]{1,0:T(2,128)} %modulation.1, bf16[1152,3456]{1,0:T(8,128)(2,1)} %w_qkv.1), custom_call_target="tpu_custom_call" | custom-call | tf_op jit(solution)/shard_map/pallas_call | solution.py:373
  79.1 2.3 %copy.11 = bf16[1,12,40,1152]{3,2,1,0:T(8,128)(2,1)} copy(bf16[1,12,40,1152]{3,2,1,0:T(8,128)(2,1)} %bitcast.6) | data formatting | bytes 2211840
  (1 shorter events, 0.0 us)

commit v3 on v2

v3 whole, which is shorter than its diff:
```python
import jax
import jax.numpy as jnp
from jax import lax
from jax.experimental import pallas as pl
from jax.experimental.pallas import tpu as pltpu
from jax.sharding import PartitionSpec as P

HEADS = 16
RADIUS = 3
NEG_FILL = -1e30
EPSILON = 1e-06
LOG2E = 1.4426950408889634
LANES = 128
UNIT = 8
MESH = pl.DeviceIdType.MESH


def head_windows(width, heads):
    size = width // heads
    last = width // LANES - 2
    found = {}
    for head in range(heads):
        tile = min(head * size // LANES, last)
        if (tile - 1) in found and (head + 1) * size <= (tile + 1) * LANES:
            tile = tile - 1
        found.setdefault(tile, []).append(head)
    return sorted(found.items())


def attend(fetch, bias, windows, size, out_ref):
    factor = size ** (-0.5) * LOG2E
    lanes = 2 * LANES

    def masks(index):
        tile, heads = windows[index]
        lane = lax.broadcasted_iota(jnp.int32, (1, lanes), 1) + tile * LANES
        return [(lane >= head * size) & (lane < (head + 1) * size) for head in heads]

    def score(index):
        query, key = fetch(0, windows[index][0]), fetch(1, windows[index][0])
        chosen = [query * jnp.where(inside, 1.0, 0.0).astype(jnp.bfloat16) for inside in masks(index)]
        return lax.dot_general(
            jnp.concatenate(chosen, 0), key, (((1,), (1,)), ((), ())), preferred_element_type=jnp.float32
        )

    following = score(0)
    for index, (tile, heads) in enumerate(windows):
        scores = following
        if index + 1 < len(windows):
            following = score(index + 1)
        count = scores.shape[0] // len(heads)
        scores = scores.reshape(len(heads), count, -1) + bias[...][None]
        top = jnp.max(scores, -1, keepdims=True)
        weights = jnp.exp2((scores - top) * factor)
        total = jnp.sum(weights, -1, keepdims=True)
        mixed = jnp.dot(
            weights.reshape(len(heads) * count, -1).astype(jnp.bfloat16),
            fetch(2, tile),
            preferred_element_type=jnp.float32,
        ).reshape(len(heads), count, lanes) * (1.0 / total)
        place = slice(tile * LANES, tile * LANES + lanes)
        current = out_ref[0:count, place]
        for number, inside in enumerate(masks(index)):
            current = jnp.where(inside, mixed[number], current)
        out_ref[0:count, place] = current


def block_kernel(
    qkv, key_keep, resid, w_out, modulation, w_qkv,
    out,
    kk, flags, kb, vb, qb, rb, wo, mo, wq, hb, he, cbias, cwin, ebias, ewin, ns, nr, tq, tb, tbias, ts,
    load_sem, col_send, col_recv, row_send, row_recv, cor_send, cor_recv,
    p1_send, p1_recv, p2_send, p2_recv, own_sem,
):
    me, row, col = lax.axis_index("tm"), lax.axis_index("row"), lax.axis_index("col")
    tm_count, row_count, col_count = (lax.axis_size(a) for a in ("tm", "row", "col"))
    _, tile_rows, tile_cols, width = qkv.shape
    size = width // HEADS
    windows = head_windows(width, HEADS)
    units = ns.shape[0]
    rounds = nr.shape[0]
    groups = tile_cols // UNIT
    middle = groups - 2
    span = 3 * RADIUS
    wide = tile_cols + 2 * UNIT
    low = tile_rows
    many, few = RADIUS * middle, RADIUS * 2
    half = 2 * (many + few)
    core_cols = pl.ds(UNIT, tile_cols)
    own_rows = pl.ds(RADIUS, tile_rows)

    loads = [
        pltpu.make_async_copy(qkv.at[1], kb.at[own_rows, core_cols, pl.ds(0, width)], load_sem.at[0]),
        pltpu.make_async_copy(key_keep, kk, load_sem.at[1]),
        pltpu.make_async_copy(qkv.at[0], qb, load_sem.at[2]),
        pltpu.make_async_copy(qkv.at[2], vb.at[own_rows, core_cols], load_sem.at[3]),
        pltpu.make_async_copy(w_out, wo, load_sem.at[4]),
        pltpu.make_async_copy(resid, rb, load_sem.at[5]),
        pltpu.make_async_copy(modulation, mo, load_sem.at[6]),
        pltpu.make_async_copy(w_qkv, wq, load_sem.at[7]),
    ]
    for load in loads[:4]:
        load.start()

    barrier = pltpu.get_barrier_semaphore()

    def greet(step, carry):
        pl.semaphore_signal(barrier, inc=1, device_id={"tm": lax.rem(me + step, tm_count)}, device_id_type=MESH)
        return carry

    lax.fori_loop(1, tm_count, greet, 0)
    for step in (1, row_count - 1):
        pl.semaphore_signal(barrier, inc=1, device_id={"row": lax.rem(row + step, row_count)}, device_id_type=MESH)
    for step in (1, col_count - 1):
        pl.semaphore_signal(barrier, inc=1, device_id={"col": lax.rem(col + step, col_count)}, device_id_type=MESH)

    def clear(rows, cols):
        for buffer in (kb, vb):
            view = buffer.at[rows, cols]
            view[...] = jnp.zeros(view.shape, view.dtype)

    everything = pl.ds(0, tile_rows + 2 * RADIUS)
    pl.when(row == 0)(lambda: clear(pl.ds(0, RADIUS), pl.ds(0, wide)))
    pl.when(row == row_count - 1)(lambda: clear(pl.ds(low + RADIUS, RADIUS), pl.ds(0, wide)))
    pl.when(col == 0)(lambda: clear(everything, pl.ds(0, UNIT)))
    pl.when(col == col_count - 1)(lambda: clear(everything, pl.ds(tile_cols + UNIT, UNIT)))
    hb[...] = jnp.zeros_like(hb)
    he[...] = jnp.zeros_like(he)
    tb[...] = jnp.zeros_like(tb)

    def window(columns):
        shape = (RADIUS * columns, span * (columns + 2 * UNIT))
        q_at = lax.broadcasted_iota(jnp.int32, shape, 0)
        k_at = lax.broadcasted_iota(jnp.int32, shape, 1)
        q_row = sum((q_at >= columns * i).astype(jnp.int32) for i in range(1, RADIUS))
        k_row = sum((k_at >= (columns + 2 * UNIT) * i).astype(jnp.int32) for i in range(1, span))
        row_gap = k_row - q_row - RADIUS
        col_gap = k_at - k_row * (columns + 2 * UNIT) - UNIT - (q_at - q_row * columns)
        near = (jnp.abs(row_gap) <= RADIUS) & (jnp.abs(col_gap) <= RADIUS)
        itself = (row_gap == 0) & (col_gap == 0)
        return jnp.where(near, 1.0, 0.0) + jnp.where(itself, 1.0, 0.0)

    cwin[...] = window(middle * UNIT)
    ewin[...] = window(UNIT)
    t_shape = tbias.shape
    same = (
        lax.broadcasted_iota(jnp.int32, t_shape, 0) - lax.broadcasted_iota(jnp.int32, t_shape, 1)
    ) & (UNIT - 1)
    tbias[...] = jnp.where(same == 0, 0.0, NEG_FILL)


    def halo(source_rows, source_cols, target_rows, target_cols, sends, recvs, target):
        copies = []
        for index, (array, buffer, lanes) in enumerate(
            ((qkv.at[1], kb, (0, width)), (flags, kb, (width, LANES)), (qkv.at[2], vb, (0, width)))
        ):
            copies.append(
                pltpu.make_async_remote_copy(
                    src_ref=array.at[source_rows, source_cols],
                    dst_ref=buffer.at[target_rows, target_cols, pl.ds(*lanes)],
                    send_sem=sends.at[index],
                    recv_sem=recvs.at[index],
                    device_id=target,
                    device_id_type=MESH,
                )
            )
        return copies

    def relay(source_cols, target_cols, rows, sends, recvs, target):
        return [
            pltpu.make_async_remote_copy(
                src_ref=buffer.at[rows, source_cols],
                dst_ref=buffer.at[rows, target_cols],
                send_sem=sends.at[index],
                recv_sem=recvs.at[index],
                device_id=target,
                device_id_type=MESH,
            )
            for index, buffer in enumerate((kb, vb))
        ]

    right = {"col": lax.rem(col + 1, col_count)}
    left = {"col": lax.rem(col + col_count - 1, col_count)}
    down = {"row": lax.rem(row + 1, row_count)}
    up = {"row": lax.rem(row + row_count - 1, row_count)}
    has = {
        "right": col < col_count - 1, "left": col > 0, "down": row < row_count - 1, "up": row > 0,
    }
    first_cols, last_cols = pl.ds(0, UNIT), pl.ds(tile_cols - UNIT, UNIT)
    left_strip, right_strip = pl.ds(0, UNIT), pl.ds(tile_cols + UNIT, UNIT)
    own_first, own_last = pl.ds(UNIT, UNIT), pl.ds(tile_cols, UNIT)
    all_rows, all_cols = pl.ds(0, tile_rows), pl.ds(0, tile_cols)
    top_halo, bottom_halo = pl.ds(0, RADIUS), pl.ds(low + RADIUS, RADIUS)
    to_right = halo(all_rows, last_cols, own_rows, left_strip, col_send.at[0], col_recv.at[0], right)
    to_left = halo(all_rows, first_cols, own_rows, right_strip, col_send.at[1], col_recv.at[1], left)
    to_down = halo(pl.ds(tile_rows - RADIUS, RADIUS), all_cols, top_halo, core_cols, row_send.at[0], row_recv.at[0], down)
    to_up = halo(pl.ds(0, RADIUS), all_cols, bottom_halo, core_cols, row_send.at[1], row_recv.at[1], up)

    def start(copies):
        for copy in copies:
            copy.start()

    def got(copies):
        for copy in copies:
            copy.wait_recv()

    def sent(copies):
        for copy in copies:
            copy.wait_send()

    corners = []
    for index, (rows, row_side) in enumerate(((top_halo, "up"), (bottom_halo, "down"))):
        corners.append(
            (relay(own_last, left_strip, rows, cor_send.at[index, 0], cor_recv.at[index, 0], right),
             has[row_side] & has["right"], has[row_side] & has["left"])
        )
        corners.append(
            (relay(own_first, right_strip, rows, cor_send.at[index, 1], cor_recv.at[index, 1], left),
             has[row_side] & has["left"], has[row_side] & has["right"])
        )

    def owner_of(unit):
        return lax.rem(unit * 5, tm_count)

    def unit_of(turn):
        return turn * tm_count + lax.rem(me * 13, tm_count)

    def place_of(unit):
        step = unit // half
        rest = unit - step * half
        central = rest < 2 * many
        past = rest - 2 * many
        pick = jnp.where(central, rest // many, past // few)
        inner = jnp.where(central, lax.rem(rest, many), lax.rem(past + few, few))
        block = jnp.where(step == 0, 1 + pick, 3 * pick)
        line = jnp.where(central, inner // middle, lax.rem(inner, RADIUS))
        group = jnp.where(central, 1 + lax.rem(inner, middle), (groups - 1) * (inner // RADIUS))
        return (block * RADIUS + line) * groups + group

    def first_copy(unit, owner):
        return pltpu.make_async_remote_copy(
            src_ref=ns.at[unit],
            dst_ref=nr.at[unit // tm_count, me],
            send_sem=p1_send,
            recv_sem=p1_recv.at[unit // tm_count],
            device_id={"tm": owner},
            device_id_type=MESH,
        )

    def second_copy(turn, unit, frame):
        return pltpu.make_async_remote_copy(
            src_ref=ts.at[turn, frame],
            dst_ref=out.at[place_of(unit)],
            send_sem=p2_send,
            recv_sem=p2_recv,
            device_id={"tm": frame},
            device_id_type=MESH,
        )

    def bias_of(live, marks):
        lane = lax.broadcasted_iota(jnp.int32, (UNIT, LANES), 1)
        pick = jnp.where(lane == 0, 1.0, 0.0).astype(jnp.bfloat16)
        keep = lax.dot_general(pick, live, (((1,), (1,)), ((), ())), preferred_element_type=jnp.float32)
        return jnp.where(marks[...] + keep[0:1] > 1.5, 0.0, NEG_FILL)

    def look(block, start_col, columns, bias, marks, target):
        first = block * RADIUS
        spread = columns + 2 * UNIT

        def fetch(kind, tile):
            lanes = slice(tile * LANES, (tile + 2) * LANES)
            if kind == 0:
                return qb[pl.ds(first, RADIUS), start_col : start_col + columns, lanes].reshape(RADIUS * columns, 2 * LANES)
            buffer = kb if kind == 1 else vb
            return buffer[pl.ds(first, span), start_col : start_col + spread, lanes].reshape(span * spread, 2 * LANES)

        live = kb[pl.ds(first, span), start_col : start_col + spread, width : width + LANES].reshape(span * spread, LANES)
        bias[...] = bias_of(live, marks)
        attend(fetch, bias, windows, size, target)

    def emit(start_unit, count, base, heads):
        stream = base.astype(jnp.float32) + jnp.dot(
            heads.astype(jnp.bfloat16), wo[...], preferred_element_type=jnp.float32
        )
        average = jnp.mean(stream, -1, keepdims=True)
        centered = stream - average
        variance = jnp.mean(centered * centered, -1, keepdims=True)
        normed = centered * lax.rsqrt(variance + EPSILON) * (1.0 + mo[1:2]) + mo[0:1]
        ns[pl.ds(start_unit, count)] = normed.astype(jnp.bfloat16).reshape(count, UNIT, width)

        def send(index, carry):
            unit = start_unit + lax.rem(index + me, count)
            owner = owner_of(unit)

            @pl.when(owner == me)
            def _():
                nr[unit // tm_count, me] = ns[unit]

            @pl.when(owner != me)
            def _():
                first_copy(unit, owner).start()

            return carry

        lax.fori_loop(0, count, send, 0)

    def temporal(turn):
        unit = unit_of(turn)

        @pl.when(unit < units)
        def _():
            arrived = nr.at[turn, pl.ds(0, tm_count - 1)]
            pltpu.make_async_copy(arrived, arrived, p1_recv.at[turn]).wait()
            rows = nr[turn].reshape(tm_count * UNIT, width)
            for part in range(9):
                place = slice(part * 3 * LANES, (part + 1) * 3 * LANES)
                tq[:, place] = jnp.dot(
                    rows, wq[:, place], preferred_element_type=jnp.float32
                ).astype(jnp.bfloat16)

            def fetch(kind, tile):
                return tq[:, kind * width + tile * LANES : kind * width + (tile + 2) * LANES]

            attend(fetch, tbias, windows, size, tb)
            ts[turn] = tb[...].astype(jnp.bfloat16).reshape(tm_count, UNIT, width)
            pltpu.make_async_copy(ts.at[turn, me], out.at[place_of(unit)], own_sem.at[turn]).start()

            def send(offset, carry):
                second_copy(turn, unit, lax.rem(me + offset, tm_count)).start()
                return carry

            lax.fori_loop(1, tm_count, send, 0)

    for load in loads[4:7]:
        load.start()
    loads[1].wait()
    eye_shape = (tile_rows, tile_cols, tile_cols)
    diagonal = lax.broadcasted_iota(jnp.int32, eye_shape, 1) == lax.broadcasted_iota(jnp.int32, eye_shape, 2)
    spread_keep = jnp.where(diagonal, kk[...].astype(jnp.float32), 0.0).reshape(tile_rows * tile_cols, tile_cols)
    along = jnp.dot(
        spread_keep.astype(jnp.bfloat16),
        jnp.ones((tile_cols, LANES), jnp.bfloat16),
        preferred_element_type=jnp.float32,
    ).astype(jnp.bfloat16).reshape(tile_rows, tile_cols, LANES)
    flags[...] = along
    kb[own_rows, UNIT : UNIT + tile_cols, width : width + LANES] = along
    pl.semaphore_wait(barrier, tm_count - 1 + 4)
    pl.when(has["right"])(lambda: start(to_right))
    pl.when(has["left"])(lambda: start(to_left))
    pl.when(has["down"])(lambda: start(to_down))
    pl.when(has["up"])(lambda: start(to_up))
    loads[7].start()
    for index in (0, 2, 3):
        loads[index].wait()

    def step_body(step, carry):
        @pl.when(step == 1)
        def _():
            pl.when(has["up"])(lambda: got(to_down))
            pl.when(has["down"])(lambda: got(to_up))
            for copies, sends, _ in corners:
                pl.when(sends)(lambda copies=copies: start(copies))

        def centre(pick, carry):
            block = jnp.where(step == 0, 1 + pick, 3 * pick)
            look(block, UNIT, middle * UNIT, cbias, cwin, hb)

            @pl.when((step == 0) & (pick == 0))
            def _():
                for load in loads[4:7]:
                    load.wait()

            rows = middle * UNIT * RADIUS
            base = rb[pl.ds(block * RADIUS, RADIUS), UNIT : (middle + 1) * UNIT].reshape(rows, width)
            emit(step * half + pick * many, many, base, hb[...])
            return carry

        lax.fori_loop(0, 2, centre, 0)

        @pl.when(step == 0)
        def _():
            pl.when(has["left"])(lambda: got(to_right))
            pl.when(has["right"])(lambda: got(to_left))

        @pl.when(step == 1)
        def _():
            for copies, _, receives in corners:
                pl.when(receives)(lambda copies=copies: got(copies))

        def edge(pick, carry):
            block = jnp.where(step == 0, 1 + pick, 3 * pick)
            look(block, 0, UNIT, ebias, ewin, he.at[0])
            look(block, tile_cols - UNIT, UNIT, ebias, ewin, he.at[1])
            rows = UNIT * RADIUS
            lines = pl.ds(block * RADIUS, RADIUS)
            base = jnp.concatenate(
                [rb[lines, 0:UNIT].astype(jnp.float32).reshape(rows, width),
                 rb[lines, tile_cols - UNIT : tile_cols].astype(jnp.float32).reshape(rows, width)], 0
            )
            emit(step * half + 2 * many + pick * few, few, base, he[...].reshape(2 * rows, width))
            return carry

        lax.fori_loop(0, 2, edge, 0)
        pl.when(step == 0)(lambda: loads[7].wait())

        def turns(index, carry):
            temporal(index)
            return carry

        lax.fori_loop(step, 1 + step * (rounds - 1), turns, 0)
        return carry

    lax.fori_loop(0, 2, step_body, 0)

    pl.when(has["right"])(lambda: sent(to_right))
    pl.when(has["left"])(lambda: sent(to_left))
    pl.when(has["down"])(lambda: sent(to_down))
    pl.when(has["up"])(lambda: sent(to_up))
    for copies, sends, _ in corners:
        pl.when(sends)(lambda copies=copies: sent(copies))

    def settle(own):
        away = pl.ds(0, units - own)
        pltpu.make_async_copy(ns.at[away], ns.at[away], p1_send).wait()
        for turn in range(own):
            pltpu.make_async_copy(ts.at[turn, me], out.at[place_of(unit_of(turn))], own_sem.at[turn]).wait()
        spent = ts.at[pl.ds(0, own), pl.ds(0, tm_count - 1)]
        pltpu.make_async_copy(spent, spent, p2_send).wait()
        pltpu.make_async_copy(out.at[away], out.at[away], p2_recv).wait()

    pl.when(unit_of(rounds - 1) < units)(lambda: settle(rounds))
    pl.when(unit_of(rounds - 1) >= units)(lambda: settle(rounds - 1))


def per_device(resid, spatial_qkv, key_keep, w_spatial_out, modulation, w_temporal_qkv):
    frame_count, tile_rows, tile_cols, width = resid.shape
    tm_count = lax.axis_size("tm")
    units = tile_rows * tile_cols // UNIT
    rounds = -(-units // tm_count)
    columns = tile_cols - 2 * UNIT
    core_rows, edge_rows = RADIUS * columns, RADIUS * UNIT
    core_keys, edge_keys = 3 * RADIUS * tile_cols, 3 * RADIUS * 3 * UNIT
    wide = tile_cols + 2 * UNIT
    pad_rows = tile_rows + 2 * RADIUS
    bf16, f32 = jnp.bfloat16, jnp.float32
    dma = pltpu.SemaphoreType.DMA
    result = pl.pallas_call(
        block_kernel,
        out_shape=jax.ShapeDtypeStruct((units, UNIT, width), bf16),
        in_specs=[pl.BlockSpec(memory_space=pltpu.HBM)] * 6,
        out_specs=pl.BlockSpec(memory_space=pl.ANY),
        scratch_shapes=[
            pltpu.VMEM((tile_rows, 1, tile_cols), jnp.int32),
            pltpu.VMEM((tile_rows, tile_cols, LANES), bf16),
            pltpu.VMEM((pad_rows, wide, width + LANES), bf16),
            pltpu.VMEM((pad_rows, wide, width), bf16),
            pltpu.VMEM((tile_rows, tile_cols, width), bf16),
            pltpu.VMEM((tile_rows, tile_cols, width), bf16),
            pltpu.VMEM((width, width), bf16),
            pltpu.VMEM((2, width), f32),
            pltpu.VMEM((width, 3 * width), bf16),
            pltpu.VMEM((core_rows, width), f32),
            pltpu.VMEM((2, edge_rows, width), f32),
            pltpu.VMEM((core_rows, core_keys), f32),
            pltpu.VMEM((core_rows, core_keys), f32),
            pltpu.VMEM((edge_rows, edge_keys), f32),
            pltpu.VMEM((edge_rows, edge_keys), f32),
            pltpu.VMEM((units, UNIT, width), bf16),
            pltpu.VMEM((rounds, tm_count, UNIT, width), bf16),
            pltpu.VMEM((tm_count * UNIT, 3 * width), bf16),
            pltpu.VMEM((tm_count * UNIT, width), f32),
            pltpu.VMEM((tm_count * UNIT, tm_count * UNIT), f32),
            pltpu.VMEM((rounds, tm_count, UNIT, width), bf16),
            dma((8,)),
            dma((2, 3)), dma((2, 3)), dma((2, 3)), dma((2, 3)), dma((2, 2, 2)), dma((2, 2, 2)),
            dma, dma((rounds,)), dma, dma, dma((rounds,)),
        ],
        compiler_params=pltpu.CompilerParams(
            collective_id=0, has_side_effects=True, vmem_limit_bytes=58 * 1024 * 1024
        ),
    )(
        spatial_qkv.reshape(3, tile_rows, tile_cols, width),
        key_keep.reshape(tile_rows, 1, tile_cols),
        resid.reshape(tile_rows, tile_cols, width),
        w_spatial_out,
        modulation,
        w_temporal_qkv,
    )
    return result.reshape(frame_count, tile_rows, tile_cols, width)


def solution(mesh):
    return jax.shard_map(
        per_device,
        mesh=mesh,
        in_specs=(
            P("tm", "row", "col", None),
            P(None, "tm", "row", "col", None),
            P("tm", "row", "col"),
            P(),
            P(),
            P(),
        ),
        out_specs=P("tm", "row", "col", None),
        check_vma=False,
    )
```

time: 81.6 us -> 68.5 us (0.84)
  Pallas kernels: 77.6 us -> 66.1 us
    pallas_call x1, Pallas kernels: 77.6 us -> 66.1 us  [per_device(): pl.pallas_call(block_kernel, out_shape=jax.ShapeDtypeStruct((units, UNIT,...]
    unnamed x2 -> x1, local copies, waits for them, and re-layouts: 2.32 us -> 2.32 us
where the time goes in v3:
time: 68.5 us; the launch traced here: 68.4 us
  Pallas kernels  66.1 us (96%)
  local copies, waits for them, and re-layouts  2.32 us (3%)
    pallas_call x1, Pallas kernels, per_device(): pl.pallas_call(block_kernel, out_shape=jax.ShapeDtypeStruct((units, UNIT,...  66.1 us
    unnamed x1, local copies, waits for them, and re-layouts  2.32 us

profile of v3, /device:TPU:1, one launch (start us, length us, event | category | flops | bytes accessed | tf_op | source)
XLA Modules:
  0.0 68.4 jit_solution(16907162349827485505)
XLA Ops:
  0.0 66.1 %shard_map.64 = bf16[60,8,1152]{2,1,0:T(8,128)(2,1)} custom-call(bf16[3,12,40,1152]{3,2,1,0:T(8,128)(2,1)} %bitcast.5, s32[12,1,40]{2,1,0:T(1,128)} %bitcast.7, bf16[12,40,1152]{2,1,0:T(8,128)(2,1)} %bitcast.6, bf16[1152,1152]{1,0:T(8,128)(2,1)} %w_out.1, f32[2,1152]{1,0:T(2,128)} %modulation.1, bf16[1152,3456]{1,0:T(8,128)(2,1)} %w_qkv.1), custom_call_target="tpu_custom_call" | custom-call | tf_op jit(solution)/shard_map/pallas_call | solution.py:447
  66.1 2.3 %copy.8 = bf16[1,12,40,1152]{3,2,1,0:T(8,128)(2,1)} copy(bf16[1,12,40,1152]{3,2,1,0:T(8,128)(2,1)} %bitcast.4) | data formatting | bytes 2211840

commit v4 on v3

--- a/solution.py
+++ b/solution.py
@@ -25,6 +25,11 @@
             tile = tile - 1
         found.setdefault(tile, []).append(head)
     return sorted(found.items())
+
+
+def far_first(count):
+    ring = count // 2
+    return sorted(range(1, count), key=lambda step: -(min(step % ring, ring - step % ring) * 2 + step // ring))
 
 
 def attend(fetch, bias, windows, size, out_ref):
@@ -68,7 +73,7 @@
 def block_kernel(
     qkv, key_keep, resid, w_out, modulation, w_qkv,
     out,
-    kk, flags, kb, vb, qb, rb, wo, mo, wq, hb, he, cbias, cwin, ebias, ewin, ns, nr, tq, tb, tbias, ts,
+    kk, flags, pack_cols, pack_cors, kb, vb, qb, rb, wo, mo, wq, hb, he, cbias, cwin, ebias, ewin, ns, nr, tq, tb, tbias, ts,
     load_sem, col_send, col_recv, row_send, row_recv, cor_send, cor_recv,
     p1_send, p1_recv, p2_send, p2_recv, own_sem,
 ):
@@ -166,18 +171,26 @@
             )
         return copies
 
-    def relay(source_cols, target_cols, rows, sends, recvs, target):
-        return [
-            pltpu.make_async_remote_copy(
-                src_ref=buffer.at[rows, source_cols],
-                dst_ref=buffer.at[rows, target_cols],
-                send_sem=sends.at[index],
-                recv_sem=recvs.at[index],
-                device_id=target,
-                device_id_type=MESH,
-            )
-            for index, buffer in enumerate((kb, vb))
-        ]
+    def pack(rows, cols, leading, target):
+        keys = kb[rows, cols, 0:width].astype(jnp.float32)
+        values = pltpu.roll(vb[rows, cols].astype(jnp.float32), 4, 1)
+        line = lax.broadcasted_iota(jnp.int32, keys.shape, 1)
+        wanted = (line < RADIUS) if leading else (line >= UNIT - RADIUS)
+        target[:, :, 0:width] = jnp.where(wanted, keys, values).astype(jnp.bfloat16)
+        target[:, :, width : width + LANES] = kb[rows, cols, width : width + LANES]
+
+    def unpack(rows, cols):
+        vb[rows, cols] = pltpu.roll(kb[rows, cols, 0:width].astype(jnp.float32), 4, 1).astype(jnp.bfloat16)
+
+    def strip(source, rows, cols, send, recv, target):
+        return pltpu.make_async_remote_copy(
+            src_ref=source,
+            dst_ref=kb.at[rows, cols],
+            send_sem=send,
+            recv_sem=recv,
+            device_id=target,
+            device_id_type=MESH,
+        )
 
     right = {"col": lax.rem(col + 1, col_count)}
     left = {"col": lax.rem(col + col_count - 1, col_count)}
@@ -186,13 +199,12 @@
     has = {
         "right": col < col_count - 1, "left": col > 0, "down": row < row_count - 1, "up": row > 0,
     }
-    first_cols, last_cols = pl.ds(0, UNIT), pl.ds(tile_cols - UNIT, UNIT)
     left_strip, right_strip = pl.ds(0, UNIT), pl.ds(tile_cols + UNIT, UNIT)
     own_first, own_last = pl.ds(UNIT, UNIT), pl.ds(tile_cols, UNIT)
-    all_rows, all_cols = pl.ds(0, tile_rows), pl.ds(0, tile_cols)
+    all_cols = pl.ds(0, tile_cols)
     top_halo, bottom_halo = pl.ds(0, RADIUS), pl.ds(low + RADIUS, RADIUS)
-    to_right = halo(all_rows, last_cols, own_rows, left_strip, col_send.at[0], col_recv.at[0], right)
-    to_left = halo(all_rows, first_cols, own_rows, right_strip, col_send.at[1], col_recv.at[1], left)
+    to_right = [strip(pack_cols.at[0], own_rows, left_strip, col_send.at[0], col_recv.at[0], right)]
+    to_left = [strip(pack_cols.at[1], own_rows, right_strip, col_send.at[1], col_recv.at[1], left)]
     to_down = halo(pl.ds(tile_rows - RADIUS, RADIUS), all_cols, top_halo, core_cols, row_send.at[0], row_recv.at[0], down)
     to_up = halo(pl.ds(0, RADIUS), all_cols, bottom_halo, core_cols, row_send.at[1], row_recv.at[1], up)
 
@@ -210,14 +222,24 @@
 
     corners = []
     for index, (rows, row_side) in enumerate(((top_halo, "up"), (bottom_halo, "down"))):
-        corners.append(
-            (relay(own_last, left_strip, rows, cor_send.at[index, 0], cor_recv.at[index, 0], right),
-             has[row_side] & has["right"], has[row_side] & has["left"])
-        )
-        corners.append(
-            (relay(own_first, right_strip, rows, cor_send.at[index, 1], cor_recv.at[index, 1], left),
-             has[row_side] & has["left"], has[row_side] & has["right"])
-        )
+        for way, (side, other, source, landing, neighbour) in enumerate(
+            (("right", "left", own_last, left_strip, right), ("left", "right", own_first, right_strip, left))
+        ):
+            place = pack_cors.at[index, way]
+            copy = strip(place, rows, landing, cor_send.at[index, way], cor_recv.at[index, way], neighbour)
+            corners.append((copy, has[row_side] & has[side], has[row_side] & has[other], rows, source, landing, place, way == 1))
+
+    def start_corner(copy, rows, source, place, leading):
+        pack(rows, source, leading, place)
+        copy.start()
+
+    def got_corner(copy, rows, landing):
+        copy.wait_recv()
+        unpack(rows, landing)
+
+    def got_strip(copies, landing):
+        got(copies)
+        unpack(own_rows, landing)
 
     def owner_of(unit):
         return lax.rem(unit * 5, tm_count)
@@ -288,21 +310,20 @@
         normed = centered * lax.rsqrt(variance + EPSILON) * (1.0 + mo[1:2]) + mo[0:1]
         ns[pl.ds(start_unit, count)] = normed.astype(jnp.bfloat16).reshape(count, UNIT, width)
 
-        def send(index, carry):
-            unit = start_unit + lax.rem(index + me, count)
-            owner = owner_of(unit)
-
-            @pl.when(owner == me)
-            def _():
-                nr[unit // tm_count, me] = ns[unit]
-
-            @pl.when(owner != me)
-            def _():
-                first_copy(unit, owner).start()
-
-            return carry
-
-        lax.fori_loop(0, count, send, 0)
+        def ahead(owner):
+            return lax.rem(owner * 13 - start_unit + 4 * tm_count, tm_count)
+
+        for offset in far_first(tm_count):
+            owner = lax.rem(me + offset, tm_count)
+
+            @pl.when(ahead(owner) < count)
+            def _(owner=owner):
+                first_copy(start_unit + ahead(owner), owner).start()
+
+        @pl.when(ahead(me) < count)
+        def _():
+            unit = start_unit + ahead(me)
+            nr[unit // tm_count, me] = ns[unit]
 
     def temporal(turn):
         unit = unit_of(turn)
@@ -325,11 +346,8 @@
             ts[turn] = tb[...].astype(jnp.bfloat16).reshape(tm_count, UNIT, width)
             pltpu.make_async_copy(ts.at[turn, me], out.at[place_of(unit)], own_sem.at[turn]).start()
 
-            def send(offset, carry):
+            for offset in far_first(tm_count):
                 second_copy(turn, unit, lax.rem(me + offset, tm_count)).start()
-                return carry
-
-            lax.fori_loop(1, tm_count, send, 0)
 
     for load in loads[4:7]:
         load.start()
@@ -344,26 +362,33 @@
     ).astype(jnp.bfloat16).reshape(tile_rows, tile_cols, LANES)
     flags[...] = along
     kb[own_rows, UNIT : UNIT + tile_cols, width : width + LANES] = along
+    for index in (0, 2, 3):
+        loads[index].wait()
+    pack(own_rows, own_last, False, pack_cols.at[0])
+    pack(own_rows, own_first, True, pack_cols.at[1])
+    look(1, UNIT, middle * UNIT, cbias, cwin, hb)
     pl.semaphore_wait(barrier, tm_count - 1 + 4)
     pl.when(has["right"])(lambda: start(to_right))
     pl.when(has["left"])(lambda: start(to_left))
     pl.when(has["down"])(lambda: start(to_down))
     pl.when(has["up"])(lambda: start(to_up))
     loads[7].start()
-    for index in (0, 2, 3):
-        loads[index].wait()
 
     def step_body(step, carry):
         @pl.when(step == 1)
         def _():
             pl.when(has["up"])(lambda: got(to_down))
             pl.when(has["down"])(lambda: got(to_up))
-            for copies, sends, _ in corners:
-                pl.when(sends)(lambda copies=copies: start(copies))
+            for copy, sends, _, rows, source, _, place, leading in corners:
+                pl.when(sends)(
+                    lambda copy=copy, rows=rows, source=source, place=place, leading=leading: start_corner(
+                        copy, rows, source, place, leading
+                    )
+                )
 
         def centre(pick, carry):
             block = jnp.where(step == 0, 1 + pick, 3 * pick)
-            look(block, UNIT, middle * UNIT, cbias, cwin, hb)
+            pl.when(step + pick > 0)(lambda: look(block, UNIT, middle * UNIT, cbias, cwin, hb))
 
             @pl.when((step == 0) & (pick == 0))
             def _():
@@ -379,13 +404,13 @@
 
         @pl.when(step == 0)
         def _():
-            pl.when(has["left"])(lambda: got(to_right))
-            pl.when(has["right"])(lambda: got(to_left))
+            pl.when(has["left"])(lambda: got_strip(to_right, left_strip))
+            pl.when(has["right"])(lambda: got_strip(to_left, right_strip))
 
         @pl.when(step == 1)
         def _():
-            for copies, _, receives in corners:
-                pl.when(receives)(lambda copies=copies: got(copies))
+            for copy, _, receives, rows, _, landing, _, _ in corners:
+                pl.when(receives)(lambda copy=copy, rows=rows, landing=landing: got_corner(copy, rows, landing))
 
         def edge(pick, carry):
             block = jnp.where(step == 0, 1 + pick, 3 * pick)
@@ -416,8 +441,8 @@
     pl.when(has["left"])(lambda: sent(to_left))
     pl.when(has["down"])(lambda: sent(to_down))
     pl.when(has["up"])(lambda: sent(to_up))
-    for copies, sends, _ in corners:
-        pl.when(sends)(lambda copies=copies: sent(copies))
+    for copy, sends, *_ in corners:
+        pl.when(sends)(lambda copy=copy: copy.wait_send())
 
     def settle(own):
         away = pl.ds(0, units - own)
@@ -452,6 +477,8 @@
         scratch_shapes=[
             pltpu.VMEM((tile_rows, 1, tile_cols), jnp.int32),
             pltpu.VMEM((tile_rows, tile_cols, LANES), bf16),
+            pltpu.VMEM((2, tile_rows, UNIT, width + LANES), bf16),
+            pltpu.VMEM((2, 2, RADIUS, UNIT, width + LANES), bf16),
             pltpu.VMEM((pad_rows, wide, width + LANES), bf16),
             pltpu.VMEM((pad_rows, wide, width), bf16),
             pltpu.VMEM((tile_rows, tile_cols, width), bf16),
@@ -472,7 +499,7 @@
             pltpu.VMEM((tm_count * UNIT, tm_count * UNIT), f32),
             pltpu.VMEM((rounds, tm_count, UNIT, width), bf16),
             dma((8,)),
-            dma((2, 3)), dma((2, 3)), dma((2, 3)), dma((2, 3)), dma((2, 2, 2)), dma((2, 2, 2)),
+            dma((2,)), dma((2,)), dma((2, 3)), dma((2, 3)), dma((2, 2)), dma((2, 2)),
             dma, dma((rounds,)), dma, dma, dma((rounds,)),
         ],
         compiler_params=pltpu.CompilerParams(

time: 68.5 us -> 65.6 us (0.958)
  Pallas kernels: 66.1 us -> 63.1 us
    pallas_call x1, Pallas kernels: 66.1 us -> 63.1 us  [per_device(): pl.pallas_call(block_kernel, out_shape=jax.ShapeDtypeStruct((units, UNIT,...]
where the time goes in v4:
time: 65.6 us; the launch traced here: 65.4 us
  Pallas kernels  63.1 us (96%)
  local copies, waits for them, and re-layouts  2.32 us (4%)
    pallas_call x1, Pallas kernels, per_device(): pl.pallas_call(block_kernel, out_shape=jax.ShapeDtypeStruct((units, UNIT,...  63.1 us
    unnamed x1, local copies, waits for them, and re-layouts  2.32 us

profile of v4, /device:TPU:1, one launch (start us, length us, event | category | flops | bytes accessed | tf_op | source)
XLA Modules:
  0.0 65.4 jit_solution(7553586258002001379)
XLA Ops:
  0.0 63.1 %shard_map.64 = bf16[60,8,1152]{2,1,0:T(8,128)(2,1)} custom-call(bf16[3,12,40,1152]{3,2,1,0:T(8,128)(2,1)} %bitcast.5, s32[12,1,40]{2,1,0:T(1,128)} %bitcast.7, bf16[12,40,1152]{2,1,0:T(8,128)(2,1)} %bitcast.6, bf16[1152,1152]{1,0:T(8,128)(2,1)} %w_out.1, f32[2,1152]{1,0:T(2,128)} %modulation.1, bf16[1152,3456]{1,0:T(8,128)(2,1)} %w_qkv.1), custom_call_target="tpu_custom_call" | custom-call | tf_op jit(solution)/shard_map/pallas_call | solution.py:472
  63.1 2.3 %copy.8 = bf16[1,12,40,1152]{3,2,1,0:T(8,128)(2,1)} copy(bf16[1,12,40,1152]{3,2,1,0:T(8,128)(2,1)} %bitcast.4) | data formatting | bytes 2211840
